TPU v7x, 256 devices: a whole 4x4x8 slice. The times are simulated.
256 devices in a mesh: space: 32 (over z, x), tm: 8 (over y, core).
Axes of the slice: x: 4, y: 4, z: 8, core: 2. Of those that a mesh axis runs over, the one named last changes fastest.
Arguments:
- iterate: float32 [8, 240, 23040], P(None, 'tm', 'space'), may hold values from -6 to 6
- residual: float32 [8, 240, 23040], P(None, 'tm', 'space'), may hold values from -24 to 24
- direction: float32 [8, 240, 23040], P(None, 'tm', 'space'), may hold values from -24 to 24
- diffusivity: float32 [23040], P('space'), may hold values from 0.1 to 0.34
- temporal_factor: float32 [240, 240], replicated, may hold values from 0 to 4
- block_tile: int32 [8, 256], P('tm', 'space'), may hold values from -1 to 479, as said below
- footprints: bfloat16 [8, 256, 64, 1440], P('tm', 'space'), may hold values from -0.15625 to 0.15625
- obs_weight: float32 [8, 32, 64], P('tm', 'space'), may hold values from 0.3 to 3
Outputs:
- iterate_next: float32 [8, 240, 23040], P(None, 'tm', 'space')
- residual_next: float32 [8, 240, 23040], P(None, 'tm', 'space')
- direction_next: float32 [8, 240, 23040], P(None, 'tm', 'space')
Inputs may be any that keep to these rules, and one draw needn't show every extreme that they name: `block_tile`: entry -1 marks a padding slot. Tile g belongs to index g // 15 of space. The valid entries of one device name distinct tiles, at most 2 of them of one owner; in each row of tm one owner is named exactly 2 times by every device.
All inputs are finite; a program needn't handle non-finite values.
Results may differ from a plain program's by a relative error of at most 0.017.
Values may be sent and summed in bfloat16 or wider, within the bound.
No kernel may reach another device: no remote copies, remote signals or barrier semaphores. Data moves between devices by JAX's collectives and lax.ppermute only.
A program may use at most 128 MiB of HBM per device.

v0:
```python
import jax
import jax.numpy as jnp
from jax import lax
from jax.sharding import PartitionSpec as P

LON = 720
TC = 48
NB = 8
DIFF = 2


def for_sending(value):

    def short(part):
        return part.astype(jnp.bfloat16) if part.dtype == jnp.float32 else part

    return jax.tree.map(short, value)


def extended_2(cells, sides, width):
    for axis, dim in sides:
        count = lax.axis_size(axis)
        ends = count - 1
        head = lax.slice_in_dim(cells, 0, width, axis=dim)
        tail = lax.slice_in_dim(cells, cells.shape[dim] - width, cells.shape[dim], axis=dim)
        cells = jnp.concatenate(
            [
                lax.ppermute(tail, axis, [(i, (i + 1) % count) for i in range(ends)]),
                cells,
                lax.ppermute(head, axis, [((i + 1) % count, i) for i in range(ends)]),
            ],
            axis=dim,
        )
    return cells


def temporal(field, matrix):
    combined = jnp.einsum(
        "tu,kuc->ktc",
        matrix,
        lax.all_to_all(
            field.astype(jnp.bfloat16), "tm", split_axis=2, concat_axis=1, tiled=True
        ).astype(field.dtype),
        precision=lax.Precision.HIGHEST,
    )
    return lax.all_to_all(
        for_sending(combined), "tm", split_axis=1, concat_axis=2, tiled=True
    ).astype(combined.dtype)


def diffuse(field, conduct):
    samples, window, cell_count = field.shape
    rows_here = cell_count // LON
    for sweep_index in range(DIFF):
        scaled_field = field * conduct
        extended = extended_2(for_sending(scaled_field), (("space", 2),), LON).astype(
            scaled_field.dtype
        )
        planes = extended.reshape(samples, window, rows_here + 2, LON)
        centre = planes[:, :, 1:-1, :]
        laplace = (
            planes[:, :, :-2, :]
            + planes[:, :, 2:, :]
            + jnp.roll(centre, 1, 3)
            + jnp.roll(centre, -1, 3)
            - 4.0 * centre
        )
        field = field + conduct * laplace.reshape(samples, window, cell_count)
    return field


def local(
    iterate, residual, direction, diffusivity, temporal_factor, block_tile, footprints, obs_weight
):
    samples, window, cell_count = direction.shape
    tiles_here = cell_count // TC
    entries = block_tile[0]
    blocks_here = entries.shape[0]
    present = entries >= 0
    mixed = temporal(direction, temporal_factor)
    spread = diffuse(mixed, diffusivity)
    tiled = spread.astype(jnp.bfloat16).reshape(samples, window, tiles_here, TC)
    empty_blocks = jnp.zeros((blocks_here, samples, window * TC), jnp.float32)
    segment = lax.all_gather(tiled, "space", axis=2, tiled=True)
    count_tiles = segment.shape[2]
    selector = (entries[:, None] == jnp.arange(count_tiles)[None, :]).astype(jnp.bfloat16)
    picked = jnp.einsum("bj,ktjc->bktc", selector, segment, preferred_element_type=jnp.float32)
    blocks = picked.reshape(empty_blocks.shape).astype(jnp.bfloat16)
    footprint = footprints[0]
    batches = obs_weight.shape[1]
    slot_obs = jnp.einsum("bmx,bkx->bkm", footprint, blocks, preferred_element_type=jnp.float32)
    batch_obs = jnp.sum(slot_obs.reshape(batches, NB, samples, footprint.shape[1]), axis=1)
    weighted = (obs_weight[0][:, None, :] * batch_obs).astype(jnp.bfloat16)
    grouped = footprint.reshape(batches, NB, footprint.shape[1], footprint.shape[2])
    gradient = jnp.einsum("anmx,akm->ankx", grouped, weighted, preferred_element_type=jnp.float32)
    gradient = gradient.reshape(blocks_here, samples, footprint.shape[2])
    gradient = jnp.where(present[:, None, None], gradient, 0.0).astype(jnp.bfloat16)
    selector = (
        entries[:, None] == jnp.arange(lax.axis_size("space") * tiles_here)[None, :]
    ).astype(jnp.bfloat16)
    summed = lax.psum_scatter(
        jnp.einsum("bj,bkx->jkx", selector, gradient, preferred_element_type=jnp.float32).astype(
            jnp.bfloat16
        ),
        "space",
        scatter_dimension=0,
        tiled=True,
    ).astype(jnp.float32)
    pulled = (
        summed.reshape(tiles_here, samples, window, TC)
        .transpose(1, 2, 0, 3)
        .reshape(samples, window, cell_count)
    )
    back = diffuse(pulled, diffusivity)
    image = direction + temporal(back, temporal_factor.T)
    old_norm, curvature = lax.psum(
        (jnp.sum(residual * residual, axis=(1, 2)), jnp.sum(direction * image, axis=(1, 2))),
        ("space", "tm"),
    )
    step_size = old_norm / curvature
    residual_next = residual - step_size[:, None, None] * image
    new_norm = lax.psum(jnp.sum(residual_next * residual_next, axis=(1, 2)), ("space", "tm"))
    iterate_next = iterate + step_size[:, None, None] * direction
    direction_next = residual_next + (new_norm / old_norm)[:, None, None] * direction
    return (iterate_next, residual_next, direction_next)


def solution(mesh):
    return jax.shard_map(
        local,
        mesh=mesh,
        in_specs=(
            P(None, "tm", "space"),
            P(None, "tm", "space"),
            P(None, "tm", "space"),
            P("space"),
            P(),
            P("tm", "space"),
            P("tm", "space", None, None),
            P("tm", "space", None),
        ),
        out_specs=(P(None, "tm", "space"), P(None, "tm", "space"), P(None, "tm", "space")),
        check_vma=False,
    )
```

profile of v0, /device:TPU:1, one launch (start us, length us, event | category | flops | bytes accessed | tf_op | source)
XLA Modules:
  0.0 832.8 jit_solution(11026537258770947451)
XLA Ops:
  7.2 1.3 convert_element_type.141
  8.5 1.5 copy.95
  10.0 2.0 reshape.151
  12.0 14.0 %all_to_all.54 = bf16[8,2,10800]{2,1,0:T(2,128)(2,1)} all-to-all(bf16[8,2,10800]{2,1,0:T(2,128)(2,1)S(1)} %reshape.151), channel_id=1, replica_groups=mesh['space'=32,'tm'=8] {'tm'}, dimensions={0} | all-to-all | bytes 691200 | tf_op jit(solution)/shard_map/all_to_all | solution.py:41
  26.0 3.1 reshape.152
  30.2 1.6 fusion.12
  32.1 12.3 %all_to_all.55 = bf16[8,240,90]{2,0,1:T(8,128)(2,1)S(1)} all-to-all(bf16[8,240,90]{2,0,1:T(8,128)(2,1)S(1)} %copy.98), channel_id=1, replica_groups=mesh['space'=32,'tm'=8] {'tm'}, dimensions={1} | all-to-all | bytes 691200 | tf_op jit(solution)/shard_map/all_to_all | solution.py:46
  45.9 1.9 multiply_convert_fusion.6
  47.8 3.4 collective-permute-start
  51.3 1.3 collective-permute-start.1
  54.9 2.8 collective-permute-done
  57.7 4.6 collective-permute-done.1
  62.3 1.3 maximum_convert_fusion
  67.5 3.1 collective-permute-start.2
  70.7 1.7 collective-permute-start.3
  72.5 1.3 copy.99
  73.8 2.7 reshape.137
  76.5 3.1 reshape.128
  81.4 1.4 maximum_convert_fusion.1
  83.1 1.2 fusion.38
  84.3 3.1 reshape.130
  87.4 4.9 fusion.5
  93.7 215.9 %all-gather.2.cloned.1.call-done = bf16[8,30,480,48]{3,0,1,2:T(8,128)(2,1)} async-done(((bf16[8,30,15,48]{3,0,1,2:T(8,128)(2,1)}), bf16[8,30,480,48]{3,0,1,2:T(8,128)(2,1)}) %all-gather.2.cloned.1.call-update) | async-done | bytes 11059216 | tf_op jit(solution)/shard_map/all_gather | solution.py:84
  309.6 26.2 %fusion.9 = bf16[8,8,30,48]{3,0,2,1:T(8,128)(2,1)S(1)} fusion(bf16[8,30,480,48]{3,0,1,2:T(8,128)(2,1)} %all-gather.2.cloned.1.call-done, s32[8]{0:T(128)S(1)} %bitcast.153), kind=kOutput, calls=%fused_computation.14 | convolution fusion | flops 88569600 | bytes 11243552 | tf_op jit(solution)/shard_map/bj,ktjc->bktc/dot_general | solution.py:87
  336.7 1.2 fusion.3
  337.9 3.7 convolution_convert_fusion
  341.6 20.4 %copy.109 = bf16[480,8,1440]{2,1,0:T(8,128)(2,1)} copy(bf16[480,8,1440]{2,0,1:T(8,128)(2,1)S(1)} %convolution_convert_fusion) | data formatting | bytes 22118400 | tf_op jit(solution)/shard_map/convert_element_type | solution.py:102
  362.1 229.4 %reduce-scatter.2.cloned.1.call-done = bf16[15,8,1440]{2,1,0:T(8,128)(2,1)} async-done(((bf16[480,8,1440]{2,1,0:T(8,128)(2,1)}), bf16[15,8,1440]{2,1,0:T(8,128)(2,1)}) %reduce-scatter.2.cloned.1.call-update) | async-done | bytes 345616 | tf_op jit(solution)/shard_map/reduce_scatter | solution.py:101
  591.4 3.0 reshape.141
  594.5 2.6 copy.110
  598.7 3.1 collective-permute-start.4
  601.8 1.3 collective-permute-start.5
  604.0 1.8 collective-permute-done.4
  605.8 4.6 collective-permute-done.5
  610.4 1.3 maximum_convert_fusion.2
  613.5 2.6 collective-permute-start.6
  616.0 1.5 collective-permute-start.7
  617.6 2.9 collective-permute-done.6
  620.5 3.8 collective-permute-done.7
  625.4 1.5 copy.112
  626.9 2.0 reshape.153
  628.9 19.2 %all_to_all.56 = bf16[8,2,10800]{2,1,0:T(2,128)(2,1)S(1)} all-to-all(bf16[8,2,10800]{2,1,0:T(2,128)(2,1)S(1)} %reshape.153), channel_id=1, replica_groups=mesh['space'=32,'tm'=8] {'tm'}, dimensions={0} | all-to-all | bytes 691200 | tf_op jit(solution)/shard_map/all_to_all | solution.py:41
  648.1 1.8 reshape.154
  651.9 12.3 %all_to_all.57 = bf16[8,240,90]{2,0,1:T(8,128)(2,1)S(1)} all-to-all(bf16[8,240,90]{2,0,1:T(8,128)(2,1)S(1)} %copy.116), channel_id=1, replica_groups=mesh['space'=32,'tm'=8] {'tm'}, dimensions={1} | all-to-all | bytes 691200 | tf_op jit(solution)/shard_map/all_to_all | solution.py:46
  666.9 81.3 %all-reduce = (f32[8]{0:T(128)S(1)}, f32[8]{0:T(128)S(1)}) all-reduce(f32[8]{0:T(128)S(1)} %get-tuple-element.31, f32[8]{0:T(128)S(1)} %get-tuple-element.7), channel_id=1, replica_groups=mesh['space'=32,'tm'=8] {'space','tm'}, use_global_device_ids=true, to_apply=%region_1.2 | all-reduce | flops 16 | bytes 128 | tf_op jit(solution)/shard_map/psum | solution.py:116
  748.2 1.5 multiply_reduce_fusion
  749.7 73.2 %psum.23 = f32[8]{0:T(128)S(1)} all-reduce(f32[8]{0:T(128)S(1)} %get-tuple-element.5), channel_id=1, replica_groups=mesh['space'=32,'tm'=8] {'space','tm'}, use_global_device_ids=true, to_apply=%region_6.7 | all-reduce | flops 8 | bytes 64 | tf_op jit(solution)/shard_map/psum | solution.py:122
  822.9 2.5 multiply_add_fusion
  (73 shorter events, 23.8 us)
Async XLA Ops:
  7.2 329.5 %copy-start = (bf16[1,8,64,1440]{3,2,1,0:T(8,128)(2,1)S(1)}, bf16[1,8,64,1440]{3,2,1,0:T(8,128)(2,1)}, u32[]{:S(2)}) copy-start(bf16[1,8,64,1440]{3,2,1,0:T(8,128)(2,1)} %param.14) | copy-start | bytes 4423684
  7.2 302.4 %all-gather.2.cloned.1.call-start = ((), (), s32[]{:S(2)}) async-start(), calls=%async_computation.5 | async-start | bytes 30412800 | tf_op jit(solution)/shard_map/all_gather | solution.py:84
  44.4 1.5 copy-start.11
  47.8 9.9 %collective-permute-start = (bf16[8,30,720]{2,0,1:T(8,128)(2,1)}, bf16[8,30,720]{2,0,1:T(8,128)(2,1)}, u32[]{:S(2)}, u32[]{:S(2)}) collective-permute-start(bf16[8,30,720]{2,0,1:T(8,128)(2,1)} %multiply_convert_fusion.6), channel_id=1, source_target_pairs={{0,8},{8,16},{16,24},{24,32},{32,40},{40,48},{48,56},{56,64},{64,7... | collective-permute-start | bytes 1036808 | tf_op jit(solution)/shard_map/ppermute | solution.py:28
  51.3 11.0 %collective-permute-start.1 = (bf16[8,30,720]{2,0,1:T(8,128)(2,1)}, bf16[8,30,720]{2,0,1:T(8,128)(2,1)}, u32[]{:S(2)}, u32[]{:S(2)}) collective-permute-start(bf16[8,30,720]{2,0,1:T(8,128)(2,1)} %multiply_convert_fusion.6), channel_id=1, source_target_pairs={{8,0},{16,8},{24,16},{32,24},{40,32},{48,40},{56,48},{64,56},{72,6... | collective-permute-start | bytes 1036808 | tf_op jit(solution)/shard_map/ppermute | solution.py:30
  63.6 1.1 copy-start.3
  64.7 2.0 copy-start.6
  65.8 0.9 copy-start.2
  67.5 12.1 %collective-permute-start.2 = (bf16[8,30,720]{2,0,1:T(8,128)(2,1)}, bf16[8,30,720]{2,0,1:T(8,128)(2,1)}, u32[]{:S(2)}, u32[]{:S(2)}) collective-permute-start(bf16[8,30,720]{2,0,1:T(8,128)(2,1)} %fusion.47), channel_id=1, source_target_pairs={{0,8},{8,16},{16,24},{24,32},{32,40},{40,48},{48,56},{56,64},{64,7... | collective-permute-start | bytes 1036808 | tf_op jit(solution)/shard_map/ppermute | solution.py:28
  70.7 9.8 %collective-permute-start.3 = (bf16[8,30,720]{2,0,1:T(8,128)(2,1)}, bf16[8,30,720]{2,0,1:T(8,128)(2,1)}, u32[]{:S(2)}, u32[]{:S(2)}) collective-permute-start(bf16[8,30,720]{2,0,1:T(8,128)(2,1)} %fusion.47), channel_id=1, source_target_pairs={{8,0},{16,8},{24,16},{32,24},{40,32},{48,40},{56,48},{64,56},{72,6... | collective-permute-start | bytes 1036808 | tf_op jit(solution)/shard_map/ppermute | solution.py:30
  92.3 1.4 copy-start.12
  93.5 498.0 %reduce-scatter.2.cloned.1.call-start = ((), (), s32[]{:S(2)}) async-start(), calls=%async_computation.6 | async-start | bytes 12165120 | tf_op jit(solution)/shard_map/reduce_scatter | solution.py:101
  309.6 27.1 %copy-start.13 = (f32[1,1,64]{2,1,0:T(1,128)S(1)}, f32[1,1,64]{2,1,0:T(1,128)}, u32[]{:S(2)}) copy-start(f32[1,1,64]{2,1,0:T(1,128)} %param.15) | copy-start | bytes 772
  598.7 7.1 collective-permute-start.4
  601.8 8.6 %collective-permute-start.5 = (bf16[8,30,720]{2,0,1:T(8,128)(2,1)}, bf16[8,30,720]{2,0,1:T(8,128)(2,1)}, u32[]{:S(2)}, u32[]{:S(2)}) collective-permute-start(bf16[8,30,720]{2,0,1:T(8,128)(2,1)} %multiply_convert_fusion.3), channel_id=1, source_target_pairs={{8,0},{16,8},{24,16},{32,24},{40,32},{48,40},{56,48},{64,56},{72,6... | collective-permute-start | bytes 1036808 | tf_op jit(solution)/shard_map/ppermute | solution.py:30
  603.9 7.7 copy-start.4
  611.8 1.1 copy-start.5
  613.5 7.0 collective-permute-start.6
  616.0 8.3 collective-permute-start.7
  648.1 2.9 copy-start.10
  664.2 1.1 copy-start.7
  664.6 1.2 copy-start.8
  749.7 75.8 %copy-start.9 = (f32[8,30,720]{2,0,1:T(8,128)}, f32[8,30,720]{2,0,1:T(8,128)S(1)}, u32[]{:S(2)}) copy-start(f32[8,30,720]{2,0,1:T(8,128)S(1)} %get-tuple-element.6) | copy-start | bytes 2073604
  822.9 2.6 copy-start.1
Sparse Core Ops, SparseCore 0:
  93.6 215.9 all-gather.1
  362.2 229.2 reduce-scatter.1
where the time goes:
time: 841 us; the launch traced here: 833 us
  waiting for transfers between devices  467 us (56%)
  blocking collectives  212 us (25%)
  local copies, waits for them, and re-layouts  62.5 us (7%)
  matrix products  33.3 us (4%)
  other arithmetic  25.1 us (3%)
  starting transfers between devices  18.3 us (2%)
  between operations  14.9 us (2%)
    reduce_scatter x1, waiting for transfers between devices, local(): lax.psum_scatter(jnp.einsum('bj,bkx->jkx', selector, gradient, preferred_...  229 us
    all_gather x1, waiting for transfers between devices, local(): segment = lax.all_gather(tiled, 'space', axis=2, tiled=True)  216 us
    psum x1, blocking collectives, local(): lax.psum((jnp.sum(residual * residual, axis=(1, 2)), jnp.sum(direction *...  81.3 us
    psum x1, blocking collectives, local(): lax.psum(jnp.sum(residual_next * residual_next, axis=(1, 2)), ('space', '...  73.2 us
    all_to_all x2, blocking collectives, temporal(): lax.all_to_all(field.astype(jnp.bfloat16), 'tm', split_axis=2, concat_axi...  33.1 us
    dot_general x1, matrix products, local(): jnp.einsum('bj,ktjc->bktc', selector, segment, preferred_element_type=jnp...  26.2 us
    all_to_all x2, blocking collectives, temporal(): lax.all_to_all(for_sending(combined), 'tm', split_axis=1, concat_axis=2,...  24.5 us
    convert_element_type x1, local copies, waits for them, and re-layouts, local(): jnp.einsum('bj,bkx->jkx', selector, gradient, preferred_element_type=jnp....  20.4 us
  transfers between devices with their start and end apart: 10, of which 9 were waited for; matrix products, arithmetic and copies ran while one was open for 1% of the time, Pallas kernels for 0%

commit v1 on v0

v1 whole, which is shorter than its diff:
```python
import jax
import jax.numpy as jnp
from jax import lax
from jax.experimental import pallas as pl
from jax.experimental.pallas import tpu as pltpu
from jax.sharding import PartitionSpec as P

LON = 720
TC = 48
NB = 8
DIFF = 2
LANES = 128
WIDE = 768
PIECES = WIDE // LANES
ROWS = 32
TW = 30
TWP = 32
NW = 8
COLS = LON // TC
BLANK = COLS * ROWS
TAIL = LON - (PIECES - 1) * LANES
IDX = 82
F32 = jnp.float32
BF16 = jnp.bfloat16


def call(body, outs, scratch=(), scalars=0):
    def run(*args):
        specs = [smem() if i < scalars else vmem() for i in range(len(args))]
        return pl.pallas_call(
            body,
            out_shape=outs,
            in_specs=specs,
            scratch_shapes=list(scratch),
            compiler_params=pltpu.CompilerParams(vmem_limit_bytes=40 * 1024 * 1024),
        )(*args)

    return run


def vmem():
    return pl.BlockSpec(memory_space=pltpu.VMEM)


def smem():
    return pl.BlockSpec(memory_space=pltpu.SMEM)


def lanes_of(shape):
    return lax.broadcasted_iota(jnp.int32, shape, len(shape) - 1)


def turn(value, shift):
    shift = shift % value.shape[-1]
    return value if shift == 0 else pltpu.roll(value, shift, value.ndim - 1)


def span(start, source, length=TC):
    parts = []
    done = 0
    while done < length:
        a, b = (source + done) // LANES, (start + done) // LANES
        take = min(length - done, (a + 1) * LANES - source - done, (b + 1) * LANES - start - done)
        low = start + done - b * LANES
        parts.append((a, b, low, low + take, (start - source) % LANES))
        done += take
    return parts


def chain(parts, lane, below=None):
    parts = sorted(parts, key=lambda part: part[0])
    result = parts[-1][2]
    for low, high, value in reversed(parts[:-1]):
        result = jnp.where(lane < high, value, result)
    return result


def prepare_body(tile_ref, d_ref, factor_ref, out_ref, hi_ref, lo_ref, z_ref, wide_ref, deep_ref, tail_ref):
    tail_ref[:, 0:TAIL] = d_ref[:, (PIECES - 1) * LANES : LON]
    lane = lanes_of((240, LANES))
    for q in range(PIECES - 1):
        z_ref[q, 0:240, :] = d_ref[:, q * LANES : (q + 1) * LANES]
        z_ref[q, 240:256, :] = jnp.zeros((16, LANES), F32)
    tail = tail_ref[...]
    first = d_ref[:, 0:LANES]
    last = jnp.where(
        lane < TAIL,
        tail,
        jnp.where(lane < TAIL + 2, turn(first, TAIL), jnp.where(lane >= LANES - 2, turn(tail, TC), 0.0)),
    )
    z_ref[PIECES - 1, 0:240, :] = last
    line = lanes_of((8, LANES))
    codes = jnp.zeros((8, LANES), F32)
    for j in range(NB):
        tile = tile_ref[0, j]
        there = tile >= 0
        safe = jnp.maximum(tile, 0)
        row = (safe * 4370) >> 16
        col = safe - row * COLS
        row = jnp.where(there, row, 0).astype(F32)
        col = jnp.where(there, col, COLS).astype(F32)
        codes = jnp.where(line == IDX + j, row, codes)
        codes = jnp.where(line == IDX + NB + j, col, codes)
    z_ref[PIECES - 1, 240:248, :] = codes
    z_ref[PIECES - 1, 248:256, :] = jnp.zeros((8, LANES), F32)
    for q in range(PIECES):
        for k in range(8):
            out_ref[k, :, q * LANES : (q + 1) * LANES] = z_ref.at[q][pl.ds(k, TWP, stride=8), :].astype(BF16)
    wide_ref[:, LANES:] = jnp.zeros((240, LANES), F32)
    wide_ref[:, 0:240] = factor_ref[...]
    factor = wide_ref[...]
    column = lanes_of((240, 256))
    padded = jnp.zeros((240, 256), F32)
    for w in range(NW):
        here = ((column >> 5) == w) & ((column & 31) < TW)
        padded = jnp.where(here, turn(factor, 2 * w), padded)
    wide_ref[...] = padded
    deep_ref[...] = jnp.zeros((256, 256), F32)
    for w in range(NW):
        deep_ref[TWP * w : TWP * w + TW, :] = wide_ref[TW * w : TW * w + TW, :]
    rows = lax.broadcasted_iota(jnp.int32, (256, 256), 0)
    column = lanes_of((256, 256))
    codes_here = ((column & 31) == TW) & ((rows >> 5) == (column >> 5)) & ((rows & 31) < TW)
    full = jnp.where(codes_here, 1.0, deep_ref[...])
    hi = full.astype(BF16)
    hi_ref[...] = hi
    lo_ref[...] = (full - hi.astype(F32)).astype(BF16)


def mix_body(x_ref, hi_ref, lo_ref, conduct_ref, out_ref, z_ref, k_ref, row_ref):
    x = x_ref[...]
    mixed = jnp.dot(hi_ref[...], x, preferred_element_type=F32) + jnp.dot(
        lo_ref[...], x, preferred_element_type=F32
    )
    for w in range(NW):
        for q in range(PIECES):
            z_ref[pl.ds(w * 8 + q, TWP, stride=64), :] = mixed[TWP * w : TWP * (w + 1), q * LANES : (q + 1) * LANES]
    lane = lanes_of((1, LANES))
    row_ref[...] = jnp.zeros((8, LANES), F32)
    row_ref[0:1, 0:TAIL] = conduct_ref[0:1, (PIECES - 1) * LANES : LON]
    tail = row_ref[0:1, :]
    first = conduct_ref[0:1, 0:LANES]
    last = jnp.where(
        lane < TAIL,
        tail,
        jnp.where(lane < TAIL + 2, turn(first, TAIL), jnp.where(lane >= LANES - 2, turn(tail, TC), 0.0)),
    )
    k_ref[...] = jnp.zeros((16, LANES), F32)
    for q in range(PIECES):
        part = last if q == PIECES - 1 else conduct_ref[0:1, q * LANES : (q + 1) * LANES]
        hi = part.astype(BF16).astype(F32)
        k_ref[q : q + 1, :] = hi
        k_ref[PIECES + q : PIECES + q + 1, :] = part - hi
    m = lax.axis_index("tm")
    for e in range(2):
        part = k_ref[pl.ds(2 * m + e, 1), :]
        z_ref[pl.ds(6 + e, 256, stride=8), :] = jnp.broadcast_to(part, (256, LANES))
    out_ref[...] = z_ref[...].astype(BF16)


def diffuse_rows(w_ref, u_ref, k_ref):
    u_ref[0] = jnp.zeros((8, WIDE), F32)
    u_ref[ROWS + 1] = jnp.zeros((8, WIDE), F32)
    for step in range(DIFF):
        for s in range(ROWS):
            u_ref[s + 1] = w_ref[s] * k_ref[s : s + 1, :]
        for s in range(ROWS):
            u = u_ref[s + 1]
            laplace = u_ref[s] + u_ref[s + 2] + turn(u, 1) + turn(u, -1) - 4.0 * u
            w_ref[s] = w_ref[s] + k_ref[s : s + 1, :] * laplace


def spread_body(slot_ref, x_ref, out_ref, kept_ref, z_ref, w_ref, u_ref, table_ref):
    z_ref[...] = x_ref[...].astype(F32)
    for q in range(PIECES):
        hi, lo = q, PIECES + q
        kept_ref[:, q * LANES : (q + 1) * LANES] = (
            z_ref[pl.ds((hi // 2) * 8 + 6 + hi % 2, ROWS, stride=64), :]
            + z_ref[pl.ds((lo // 2) * 8 + 6 + lo % 2, ROWS, stride=64), :]
        )
        for s in range(ROWS):
            w_ref[s, :, q * LANES : (q + 1) * LANES] = z_ref[pl.ds(s * 64 + q, 8, stride=8), :]
    diffuse_rows(w_ref, u_ref, kept_ref)
    lane = lanes_of((8, LANES))
    for s in range(ROWS):
        for c in range(COLS):
            parts = [
                (low, high, turn(w_ref[s, :, a * LANES : (a + 1) * LANES], rotation))
                for a, _, low, high, rotation in span(0, c * TC)
            ]
            table_ref[c * ROWS + s] = chain(parts, lane)
    table_ref[BLANK] = jnp.zeros((8, LANES), F32)

    def reader(s, carry):
        runs = [[], [], []]
        for j in range(NB):
            tile = table_ref[slot_ref[s * NB + j]]
            for _, b, low, high, rotation in span(j * TC, 0):
                runs[b].append((low, high, turn(tile, rotation)))
        for b in range(3):
            out_ref[s, :, b * LANES : (b + 1) * LANES] = chain(runs[b], lane).astype(BF16)
        return carry

    lax.fori_loop(0, ROWS, reader, 0)


def observe_body(x_ref, f_ref, weight_ref, out_ref, x2_ref, g_ref):
    lane = lanes_of((8, LANES))
    runs = {}
    for tau in range(TW):
        value = x_ref[tau].astype(F32)
        for j in range(NB):
            for a, b, low, high, rotation in span(tau * TC, j * TC):
                piece = turn(value[:, a * LANES : (a + 1) * LANES], rotation)
                runs.setdefault((j, b), []).append((low, high, piece))
        for key in [key for key in runs if (key[1] + 1) * LANES <= (tau + 1) * TC or tau == TW - 1]:
            j, b = key
            x2_ref[j, :, b * LANES : (b + 1) * LANES] = chain(runs.pop(key), lane)
    total = jnp.zeros((8, 64), F32)
    for j in range(NB):
        total = total + lax.dot_general(
            x2_ref[j, :, 0 : TW * TC].astype(BF16),
            f_ref[j],
            (((1,), (1,)), ((), ())),
            preferred_element_type=F32,
        )
    weighted = (weight_ref[...] * total).astype(BF16)
    for j in range(NB):
        g_ref[j, :, 0 : TW * TC] = jnp.dot(weighted, f_ref[j], preferred_element_type=F32)
    for tau in range(TW):
        runs = [[], [], []]
        for j in range(NB):
            for a, b, low, high, rotation in span(j * TC, tau * TC):
                runs[b].append((low, high, turn(g_ref[j, :, a * LANES : (a + 1) * LANES], rotation)))
        for b in range(3):
            out_ref[tau, :, b * LANES : (b + 1) * LANES] = chain(runs[b], lane).astype(BF16)
    out_ref[TW:TWP] = jnp.zeros((TWP - TW, 8, NB * TC), BF16)


def collect_body(slot_ref, x_ref, k_ref, out_ref, z_ref, w_ref, u_ref, table_ref):
    lane = lanes_of((8, LANES))
    table_ref[...] = jnp.zeros(table_ref.shape, F32)

    def reader(s, carry):
        value = x_ref[s].astype(F32)
        for j in range(NB):
            parts = [
                (low, high, turn(value[:, a * LANES : (a + 1) * LANES], rotation))
                for a, _, low, high, rotation in span(0, j * TC)
            ]
            g = slot_ref[s * NB + j]
            table_ref[g] = table_ref[g] + chain(parts, lane)
        return carry

    lax.fori_loop(0, ROWS, reader, 0)
    for s in range(ROWS):
        runs = [[] for _ in range(PIECES)]
        for c in range(COLS):
            tile = table_ref[c * ROWS + s]
            for _, b, low, high, rotation in span(c * TC, 0):
                runs[b].append((low, high, turn(tile, rotation)))
        runs[-1].append((TAIL, TAIL + 2, turn(table_ref[s], TAIL)))
        runs[-1].append((TAIL + 2, LANES - 2, jnp.zeros((8, LANES), F32)))
        runs[-1].append((LANES - 2, LANES, turn(table_ref[(COLS - 1) * ROWS + s], TAIL)))
        for b in range(PIECES):
            w_ref[s, :, b * LANES : (b + 1) * LANES] = chain(runs[b], lane)
    diffuse_rows(w_ref, u_ref, k_ref)
    for s in range(ROWS):
        for q in range(PIECES):
            z_ref[pl.ds(s * 64 + q, 8, stride=8), :] = w_ref[s, :, q * LANES : (q + 1) * LANES]
        for q in range(PIECES, 8):
            z_ref[pl.ds(s * 64 + q, 8, stride=8), :] = jnp.zeros((8, LANES), F32)
    out_ref[...] = z_ref[...].astype(BF16)


def unmix_body(x_ref, hi_ref, lo_ref, out_ref, z_ref, w_ref):
    z_ref[...] = x_ref[...].astype(F32)
    for w in range(NW):
        for q in range(PIECES):
            w_ref[TWP * w : TWP * (w + 1), q * LANES : (q + 1) * LANES] = z_ref[
                pl.ds(w * 8 + q, TWP, stride=64), :
            ].astype(BF16)
    x = w_ref[...]
    down = (((0,), (0,)), ((), ()))
    mixed = lax.dot_general(hi_ref[...], x, down, preferred_element_type=F32) + lax.dot_general(
        lo_ref[...], x, down, preferred_element_type=F32
    )
    out_ref[...] = mixed.astype(BF16)


def image_body(x_ref, d_ref, r_ref, image_ref, sums_ref, z_ref):
    for q in range(PIECES):
        z_ref[q] = x_ref[:, q * LANES : (q + 1) * LANES].astype(F32)
    totals = [jnp.zeros((8, 1), F32) for _ in range(4)]
    for q in range(PIECES):
        width = TAIL if q == PIECES - 1 else LANES
        at = pl.ds(q * LANES, width)
        sums = [jnp.zeros((8, width), F32) for _ in range(4)]
        for t in range(TW):
            d = d_ref[t, :, at]
            r = r_ref[t, :, at]
            image = d + z_ref.at[q][pl.ds(t, 8, stride=TWP), :][:, 0:width]
            image_ref[t, :, at] = image
            for i, (left, right) in enumerate(((r, r), (d, image), (r, image), (image, image))):
                sums[i] = sums[i] + left * right
        for i in range(4):
            totals[i] = totals[i] + jnp.sum(sums[i], axis=1, keepdims=True)
    lane = lanes_of((8, LANES))
    k = lax.broadcasted_iota(jnp.int32, (8, LANES), 0)
    spread = jnp.zeros((8, LANES), F32)
    for i in range(4):
        spread = jnp.where(lane == k * 4 + i, totals[i], spread)
    line = jnp.sum(spread, axis=0, keepdims=True)
    sums_ref[...] = jnp.broadcast_to(line, sums_ref.shape)


def update_body(sums_ref, it_ref, r_ref, d_ref, image_ref, it_out, r_out, d_out):
    line = jnp.sum(sums_ref[...], axis=0, keepdims=True)
    lane = lanes_of((8, LANES))
    k = lax.broadcasted_iota(jnp.int32, (8, LANES), 0)
    rr, dq, rq, qq = [
        jnp.sum(jnp.where(lane == k * 4 + i, line, 0.0), axis=1, keepdims=True) for i in range(4)
    ]
    step = rr / dq
    norm = jnp.maximum(rr + step * (step * qq - 2.0 * rq), 0.0)
    ratio = norm / rr
    for t in range(TW):
        d = d_ref[t]
        after = r_ref[t] - step * image_ref[t]
        it_out[t] = it_ref[t] + step * d
        r_out[t] = after
        d_out[t] = after + ratio * d


def shape(dims, dtype):
    return jax.ShapeDtypeStruct(dims, dtype)


def local(
    iterate, residual, direction, diffusivity, temporal_factor, block_tile, footprints, obs_weight
):
    both = ("space", "tm")
    iterate, residual, direction = [
        jnp.transpose(value, (1, 0, 2)) for value in (iterate, residual, direction)
    ]
    grid = (ROWS, 8, WIDE)
    with jax.named_scope("prepare"):
        message, hi, lo = call(
            prepare_body,
            (shape((8, TWP, WIDE), BF16), shape((256, 256), BF16), shape((256, 256), BF16)),
            [
                pltpu.VMEM((PIECES, 256, LANES), F32),
                pltpu.VMEM((240, 256), F32),
                pltpu.VMEM((256, 256), F32),
                pltpu.VMEM((240, LANES), F32),
            ],
            1,
        )(block_tile, direction.reshape(240, LON), temporal_factor)
        message = lax.all_to_all(message, "tm", 0, 0, tiled=True)
    with jax.named_scope("mix"):
        message = call(
            mix_body,
            shape((2048, LANES), BF16),
            [pltpu.VMEM((2048, LANES), F32), pltpu.VMEM((16, LANES), F32), pltpu.VMEM((8, LANES), F32)],
        )(message.reshape(256, WIDE), hi, lo, diffusivity.reshape(1, LON))
        message = lax.all_to_all(message.reshape(256, 8, LANES), both, 0, 0, tiled=True)
    with jax.named_scope("slots"):
        codes = message.reshape(ROWS, 8, 8, LANES)[:, 0, PIECES - 1, IDX : IDX + 2 * NB].astype(F32)
        slots = (codes[:, NB:] * ROWS + codes[:, :NB]).astype(jnp.int32).reshape(ROWS * NB)
    with jax.named_scope("spread"):
        message, conduct = call(
            spread_body,
            (shape((ROWS, 8, NB * TC), BF16), shape((ROWS, WIDE), F32)),
            [
                pltpu.VMEM((2048, LANES), F32),
                pltpu.VMEM(grid, F32),
                pltpu.VMEM((ROWS + 2, 8, WIDE), F32),
                pltpu.VMEM((BLANK + 1, 8, LANES), F32),
            ],
            1,
        )(slots, message.reshape(2048, LANES))
        message = lax.all_to_all(message, "space", 0, 0, tiled=True)
    with jax.named_scope("observe"):
        message = call(
            observe_body,
            shape((TWP, 8, NB * TC), BF16),
            [pltpu.VMEM((NB, 8, 1536), F32), pltpu.VMEM((NB, 8, 1536), F32)],
        )(message, footprints[0], obs_weight[0])
        message = lax.all_to_all(message, "space", 0, 0, tiled=True)
    with jax.named_scope("collect"):
        message = call(
            collect_body,
            shape((2048, LANES), BF16),
            [
                pltpu.VMEM((2048, LANES), F32),
                pltpu.VMEM(grid, F32),
                pltpu.VMEM((ROWS + 2, 8, WIDE), F32),
                pltpu.VMEM((BLANK + 1, 8, LANES), F32),
            ],
            1,
        )(slots, message, conduct)
        message = lax.all_to_all(message.reshape(256, 8, LANES), both, 0, 0, tiled=True)
    with jax.named_scope("unmix"):
        message = call(
            unmix_body,
            shape((256, WIDE), BF16),
            [pltpu.VMEM((2048, LANES), F32), pltpu.VMEM((256, WIDE), BF16)],
        )(message.reshape(2048, LANES), hi, lo)
        message = lax.all_to_all(message.reshape(8, TWP, WIDE), "tm", 0, 0, tiled=True)
    with jax.named_scope("image"):
        image, sums = call(
            image_body,
            (shape((TW, 8, LON), F32), shape((256, LANES), F32)),
            [pltpu.VMEM((PIECES, 256, LANES), F32)],
        )(message.reshape(256, WIDE), direction, residual)
        sums = lax.all_to_all(sums, both, 0, 0, tiled=True)
    with jax.named_scope("update"):
        outs = call(update_body, tuple(shape((TW, 8, LON), F32) for _ in range(3)))(
            sums, iterate, residual, direction, image
        )
    return tuple(jnp.transpose(value, (1, 0, 2)) for value in outs)


def solution(mesh):
    return jax.shard_map(
        local,
        mesh=mesh,
        in_specs=(
            P(None, "tm", "space"),
            P(None, "tm", "space"),
            P(None, "tm", "space"),
            P("space"),
            P(),
            P("tm", "space"),
            P("tm", "space", None, None),
            P("tm", "space", None),
        ),
        out_specs=(P(None, "tm", "space"), P(None, "tm", "space"), P(None, "tm", "space")),
        check_vma=False,
    )
```

time: 841 us -> 156 us (0.19)
  waiting for transfers between devices: 467 us -> 8.09 us
  blocking collectives: 212 us -> 120 us
  local copies, waits for them, and re-layouts: 62.5 us -> 2.83 us
  matrix products: 33.3 us -> 0 us
  other arithmetic: 25.1 us -> 0.17 us
  Pallas kernels: 0 us -> 17.2 us
  between operations: 14.9 us -> 0.71 us
  starting transfers between devices: 18.3 us -> 6.6 us
    reduce_scatter x1 -> x0, waiting for transfers between devices: 229 us -> none  [local(): lax.psum_scatter(jnp.einsum('bj,bkx->jkx', selector, gradient, preferred_...]
    all_gather x1 -> x0, waiting for transfers between devices: 216 us -> none  [local(): segment = lax.all_gather(tiled, 'space', axis=2, tiled=True)]
    psum x2 -> x0, blocking collectives: 155 us -> none  [the longest x1 81.3 us: local(): lax.psum((jnp.sum(residual * residual, axis=(1, 2)), jnp.sum(direction *...]
    all_to_all x4 -> x6, blocking collectives: 57.7 us -> 120 us  [the longest x2 60.1 us: local(): lax.all_to_all(message.reshape(256, 8, LANES), both, 0, 0, tiled=True)]
    convert_element_type x15 -> x0, local copies, waits for them, and re-layouts: 33.4 us -> none  [the longest x1 20.4 us: local(): jnp.einsum('bj,bkx->jkx', selector, gradient, preferred_element_type=jnp....]
    dot_general x5 -> x0, matrix products: 33.3 us -> none  [the longest x1 26.2 us: local(): jnp.einsum('bj,ktjc->bktc', selector, segment, preferred_element_type=jnp...]
    ppermute x8 -> x0, waiting for transfers between devices: 21.3 us -> none  [the longest x4 13.8 us: extended_2(): lax.ppermute(head, axis, [((i + 1) % count, i) for i in range(ends)])]
    ppermute x8 -> x0, starting transfers between devices: 18 us -> none  [the longest x4 12.2 us: extended_2(): lax.ppermute(tail, axis, [(i, (i + 1) % count) for i in range(ends)])]
  transfers between devices with their start and end apart: 10 -> 1, of which waited for: 9 -> 1; matrix products, arithmetic and copies ran while one was open for 1% -> 0% of each run, Pallas kernels for 0% -> 0%
where the time goes in v1:
time: 156 us; the launch traced here: 155 us
  blocking collectives  120 us (77%)
  Pallas kernels  17.2 us (11%)
  waiting for transfers between devices  8.09 us (5%)
  starting transfers between devices  6.6 us (4%)
  local copies, waits for them, and re-layouts  2.83 us (2%)
    all_to_all x2, blocking collectives, local(): lax.all_to_all(message.reshape(256, 8, LANES), both, 0, 0, tiled=True)  60.1 us
    all_to_all x2, blocking collectives, local(): message = lax.all_to_all(message, 'space', 0, 0, tiled=True)  28.4 us
    all_to_all x1, blocking collectives, local(): sums = lax.all_to_all(sums, both, 0, 0, tiled=True)  18.7 us
    pallas_call x8, Pallas kernels, run(): pl.pallas_call(body, out_shape=outs, in_specs=specs, scratch_shapes=list(...  17.2 us
    all_to_all x1, blocking collectives, local(): lax.all_to_all(message.reshape(8, TWP, WIDE), 'tm', 0, 0, tiled=True)  12.6 us
    all_to_all x1, waiting for transfers between devices, local(): message = lax.all_to_all(message, 'tm', 0, 0, tiled=True)  8.09 us
    all_to_all x1, starting transfers between devices, local(): message = lax.all_to_all(message, 'tm', 0, 0, tiled=True)  6.6 us
  transfers between devices with their start and end apart: 1, of which 1 were waited for; matrix products, arithmetic and copies ran while one was open for 0% of the time, Pallas kernels for 0%

profile of v1, /device:TPU:1, one launch (start us, length us, event | category | flops | bytes accessed | tf_op | source)
XLA Modules:
  0.0 155.5 jit_solution(13218002628554642503)
XLA Ops:
  0.6 0.0 copy-start
  0.6 1.1 copy-done
  1.8 0.0 copy-start.5
  1.8 0.9 copy-done.5
  2.7 0.0 copy-start.6
  2.7 0.7 copy-done.6
  3.4 0.0 copy-start.8
  3.4 2.1 %prepare.1 = (bf16[8,32,768]{2,1,0:T(8,128)(2,1)}, bf16[256,256]{1,0:T(8,128)(2,1)S(1)}, bf16[256,256]{1,0:T(8,128)(2,1)S(1)}) custom-call(s32[1,8]{1,0:T(1,128)S(1)} %copy-done.6, f32[240,720]{1,0:T(8,128)S(1)} %bitcast.23, f32[240,240]{1,0:T(8,128)S(1)} %copy-done.5), custom_call_target="tpu_custom_call" | custom-call | tf_op jit(solution)/shard_map/prepare/pallas_call | solution.py:30
  5.5 6.6 %all-to-all-start = ((bf16[8,32,768]{2,1,0:T(8,128)(2,1)}), bf16[8,32,768]{2,1,0:T(8,128)(2,1)S(1)}, u32[]{:S(2)}, u32[]{:S(2)}) async-start(bf16[8,32,768]{2,1,0:T(8,128)(2,1)} %get-tuple-element.13), calls=%async_computation | async-start | bytes 786432 | tf_op jit(solution)/shard_map/prepare/all_to_all | solution.py:359
  12.1 0.0 copy-done.8
  12.1 8.1 %all-to-all-done = bf16[8,32,768]{2,1,0:T(8,128)(2,1)S(1)} async-done(((bf16[8,32,768]{2,1,0:T(8,128)(2,1)}), bf16[8,32,768]{2,1,0:T(8,128)(2,1)S(1)}, u32[]{:S(2)}, u32[]{:S(2)}) %all-to-all-start) | async-done | bytes 393248 | tf_op jit(solution)/shard_map/prepare/all_to_all | solution.py:359
  20.2 0.0 copy-start.3
  20.2 0.0 copy-start.7
  20.2 0.9 mix.1
  21.1 32.1 %all_to_all.41 = bf16[256,8,128]{2,1,0:T(8,128)(2,1)S(1)} all-to-all(bf16[256,8,128]{2,1,0:T(8,128)(2,1)S(1)} %bitcast.32), channel_id=1, replica_groups=mesh['space'=32,'tm'=8] {'space','tm'}, dimensions={0} | all-to-all | bytes 1048576 | tf_op jit(solution)/shard_map/mix/all_to_all | solution.py:366
  53.2 0.1 slice_convert_fusion
  53.3 0.1 fusion
  53.4 0.1 reshape.48.slot_ref
  53.4 4.6 %spread.1 = (bf16[32,8,384]{2,1,0:T(8,128)(2,1)S(1)}, f32[32,768]{1,0:T(8,128)S(1)}) custom-call(s32[256]{0:T(256)S(1)} %reshape.48.slot_ref, bf16[2048,128]{1,0:T(8,128)(2,1)S(1)} %bitcast.29), custom_call_target="tpu_custom_call" | custom-call | tf_op jit(solution)/shard_map/spread/pallas_call | solution.py:30
  58.0 14.1 %all_to_all.42.x_ref = bf16[32,8,384]{2,1,0:T(8,128)(2,1)S(1)} all-to-all(bf16[32,8,384]{2,1,0:T(8,128)(2,1)S(1)} %get-tuple-element.16), channel_id=1, replica_groups=mesh['space'=32,'tm'=8] {'space'}, dimensions={0} | all-to-all | bytes 393216 | tf_op jit(solution)/shard_map/spread/all_to_all | solution.py:382
  72.1 0.0 copy-done.3
  72.1 0.0 copy-done.7
  72.1 1.4 observe.1
  73.5 14.3 %all_to_all.43.x_ref = bf16[32,8,384]{2,1,0:T(8,128)(2,1)S(1)} all-to-all(bf16[32,8,384]{2,1,0:T(8,128)(2,1)S(1)} %observe.1), channel_id=1, replica_groups=mesh['space'=32,'tm'=8] {'space'}, dimensions={0} | all-to-all | bytes 393216 | tf_op jit(solution)/shard_map/observe/all_to_all | solution.py:389
  87.9 5.1 %collect.1 = bf16[2048,128]{1,0:T(8,128)(2,1)S(1)} custom-call(s32[256]{0:T(256)S(1)} %reshape.48.slot_ref, bf16[32,8,384]{2,1,0:T(8,128)(2,1)S(1)} %all_to_all.43.x_ref, f32[32,768]{1,0:T(8,128)S(1)} %get-tuple-element.17.k_ref), custom_call_target="tpu_custom_call" | custom-call | tf_op jit(solution)/shard_map/collect/pallas_call | solution.py:30
  92.9 0.0 copy-start.1
  93.0 0.0 copy-start.2
  93.0 28.0 %all_to_all.44 = bf16[256,8,128]{2,1,0:T(8,128)(2,1)S(1)} all-to-all(bf16[256,8,128]{2,1,0:T(8,128)(2,1)S(1)} %bitcast.30), channel_id=1, replica_groups=mesh['space'=32,'tm'=8] {'space','tm'}, dimensions={0} | all-to-all | bytes 1048576 | tf_op jit(solution)/shard_map/collect/all_to_all | solution.py:402
  121.0 0.9 unmix.1
  121.9 0.0 copy-start.4
  121.9 12.6 %all_to_all.45 = bf16[8,32,768]{2,1,0:T(8,128)(2,1)S(1)} all-to-all(bf16[8,32,768]{2,1,0:T(8,128)(2,1)S(1)} %bitcast.36), channel_id=1, replica_groups=mesh['space'=32,'tm'=8] {'tm'}, dimensions={0} | all-to-all | bytes 786432 | tf_op jit(solution)/shard_map/unmix/all_to_all | solution.py:409
  134.5 0.0 copy-done.1
  134.5 0.0 copy-done.2
  134.5 0.7 image.1
  135.2 18.7 %all_to_all.46 = f32[256,1,128]{2,1,0:T(1,128)S(1)} all-to-all(f32[256,1,128]{2,1,0:T(1,128)S(1)} %bitcast.39), channel_id=1, replica_groups=mesh['space'=32,'tm'=8] {'space','tm'}, dimensions={0} | all-to-all | bytes 262144 | tf_op jit(solution)/shard_map/image/all_to_all | solution.py:416
  153.9 0.0 copy-done.4
  153.9 1.6 %update.1 = (f32[30,8,720]{2,1,0:T(8,128)}, f32[30,8,720]{2,1,0:T(8,128)}, f32[30,8,720]{2,1,0:T(8,128)}) custom-call(f32[256,128]{1,0:T(8,128)S(1)} %bitcast.38, f32[30,8,720]{2,1,0:T(8,128)S(1)} %bitcast.37, f32[30,8,720]{2,1,0:T(8,128)S(1)} %bitcast.27, f32[30,8,720]{2,1,0:T(8,128)S(1)} %bitcast.25, f32[30,8,720]{2,1,0:T(8,128)S(1)} %get-tuple-element.19.image_ref), custom_call_target="tpu_custom_call" | custom-call | tf_op jit(solution)/shard_map/update/pallas_call | solution.py:30
  (1 shorter events, 0.0 us)
Async XLA Ops:
  0.6 1.1 copy-start
  1.8 0.9 copy-start.5
  2.7 0.7 copy-start.6
  3.4 8.7 %copy-start.8 = (f32[720]{0:T(1024)S(1)}, f32[720]{0:T(1024)}, u32[]{:S(2)}) copy-start(f32[720]{0:T(1024)} %param.11) | copy-start | bytes 8644
  5.5 14.7 %all-to-all-start = ((bf16[8,32,768]{2,1,0:T(8,128)(2,1)}), bf16[8,32,768]{2,1,0:T(8,128)(2,1)S(1)}, u32[]{:S(2)}, u32[]{:S(2)}) async-start(bf16[8,32,768]{2,1,0:T(8,128)(2,1)} %get-tuple-element.13), calls=%async_computation | async-start | bytes 786432 | tf_op jit(solution)/shard_map/prepare/all_to_all | solution.py:359
  20.2 52.0 %copy-start.3 = (bf16[1,8,64,1440]{3,2,1,0:T(8,128)(2,1)S(1)}, bf16[1,8,64,1440]{3,2,1,0:T(8,128)(2,1)}, u32[]{:S(2)}) copy-start(bf16[1,8,64,1440]{3,2,1,0:T(8,128)(2,1)} %param.14) | copy-start | bytes 4423684
  20.2 52.0 %copy-start.7 = (f32[1,1,64]{2,1,0:T(1,128)S(1)}, f32[1,1,64]{2,1,0:T(1,128)}, u32[]{:S(2)}) copy-start(f32[1,1,64]{2,1,0:T(1,128)} %param.15) | copy-start | bytes 772
  92.9 41.6 %copy-start.1 = (f32[8,30,720]{2,0,1:T(8,128)S(1)}, f32[8,30,720]{2,0,1:T(8,128)}, u32[]{:S(2)}) copy-start(f32[8,30,720]{2,0,1:T(8,128)} %param.10) | copy-start | bytes 2073604
  93.0 41.6 %copy-start.2 = (f32[8,30,720]{2,0,1:T(8,128)S(1)}, f32[8,30,720]{2,0,1:T(8,128)}, u32[]{:S(2)}) copy-start(f32[8,30,720]{2,0,1:T(8,128)} %param.9) | copy-start | bytes 2073604
  121.9 32.0 %copy-start.4 = (f32[8,30,720]{2,0,1:T(8,128)S(1)}, f32[8,30,720]{2,0,1:T(8,128)}, u32[]{:S(2)}) copy-start(f32[8,30,720]{2,0,1:T(8,128)} %param.8) | copy-start | bytes 2073604

commit v2 on v1

--- a/solution.py
+++ b/solution.py
@@ -24,26 +24,24 @@
 BF16 = jnp.bfloat16
 
 
-def call(body, outs, scratch=(), scalars=0):
+def call(body, outs, scratch=(), places="", out_places=None):
+    space = {"v": pltpu.VMEM, "s": pltpu.SMEM, "h": pltpu.HBM}
+
     def run(*args):
-        specs = [smem() if i < scalars else vmem() for i in range(len(args))]
+        kinds = places + "v" * (len(args) - len(places))
+        more = {}
+        if out_places is not None:
+            more["out_specs"] = tuple(pl.BlockSpec(memory_space=space[kind]) for kind in out_places)
         return pl.pallas_call(
             body,
             out_shape=outs,
-            in_specs=specs,
+            in_specs=[pl.BlockSpec(memory_space=space[kind]) for kind in kinds],
             scratch_shapes=list(scratch),
             compiler_params=pltpu.CompilerParams(vmem_limit_bytes=40 * 1024 * 1024),
+            **more,
         )(*args)
 
     return run
-
-
-def vmem():
-    return pl.BlockSpec(memory_space=pltpu.VMEM)
-
-
-def smem():
-    return pl.BlockSpec(memory_space=pltpu.SMEM)
 
 
 def lanes_of(shape):
@@ -75,20 +73,35 @@
     return result
 
 
-def prepare_body(tile_ref, d_ref, factor_ref, out_ref, hi_ref, lo_ref, z_ref, wide_ref, deep_ref, tail_ref):
-    tail_ref[:, 0:TAIL] = d_ref[:, (PIECES - 1) * LANES : LON]
-    lane = lanes_of((240, LANES))
+def prepare_body(tile_hbm, d_hbm, out_ref, z_ref, d_ref, tail_ref, tile_ref, sem, tile_sem):
+    count = 6
+    rows = 240 // count
+    copies = [
+        pltpu.make_async_copy(d_hbm.at[pl.ds(i * rows, rows)], d_ref.at[pl.ds(i * rows, rows)], sem.at[i])
+        for i in range(count)
+    ]
+    tile_copy = pltpu.make_async_copy(tile_hbm, tile_ref, tile_sem)
+    for copy in copies:
+        copy.start()
+    tile_copy.start()
+    lane = lanes_of((rows, LANES))
     for q in range(PIECES - 1):
-        z_ref[q, 0:240, :] = d_ref[:, q * LANES : (q + 1) * LANES]
         z_ref[q, 240:256, :] = jnp.zeros((16, LANES), F32)
-    tail = tail_ref[...]
-    first = d_ref[:, 0:LANES]
-    last = jnp.where(
-        lane < TAIL,
-        tail,
-        jnp.where(lane < TAIL + 2, turn(first, TAIL), jnp.where(lane >= LANES - 2, turn(tail, TC), 0.0)),
-    )
-    z_ref[PIECES - 1, 0:240, :] = last
+    z_ref[PIECES - 1, 248:256, :] = jnp.zeros((8, LANES), F32)
+    for i in range(count):
+        copies[i].wait()
+        at = pl.ds(i * rows, rows)
+        tail_ref[at, 0:TAIL] = d_ref[at, (PIECES - 1) * LANES : LON]
+        for q in range(PIECES - 1):
+            z_ref[q, at, :] = d_ref[at, q * LANES : (q + 1) * LANES]
+        tail = tail_ref[at, :]
+        first = d_ref[at, 0:LANES]
+        z_ref[PIECES - 1, at, :] = jnp.where(
+            lane < TAIL,
+            tail,
+            jnp.where(lane < TAIL + 2, turn(first, TAIL), jnp.where(lane >= LANES - 2, turn(tail, TC), 0.0)),
+        )
+    tile_copy.wait()
     line = lanes_of((8, LANES))
     codes = jnp.zeros((8, LANES), F32)
     for j in range(NB):
@@ -102,10 +115,12 @@
         codes = jnp.where(line == IDX + j, row, codes)
         codes = jnp.where(line == IDX + NB + j, col, codes)
     z_ref[PIECES - 1, 240:248, :] = codes
-    z_ref[PIECES - 1, 248:256, :] = jnp.zeros((8, LANES), F32)
     for q in range(PIECES):
         for k in range(8):
             out_ref[k, :, q * LANES : (q + 1) * LANES] = z_ref.at[q][pl.ds(k, TWP, stride=8), :].astype(BF16)
+
+
+def factor_body(factor_ref, hi_ref, lo_ref, wide_ref, deep_ref):
     wide_ref[:, LANES:] = jnp.zeros((240, LANES), F32)
     wide_ref[:, 0:240] = factor_ref[...]
     factor = wide_ref[...]
@@ -158,19 +173,28 @@
     out_ref[...] = z_ref[...].astype(BF16)
 
 
-def diffuse_rows(w_ref, u_ref, k_ref):
-    u_ref[0] = jnp.zeros((8, WIDE), F32)
-    u_ref[ROWS + 1] = jnp.zeros((8, WIDE), F32)
-    for step in range(DIFF):
-        for s in range(ROWS):
-            u_ref[s + 1] = w_ref[s] * k_ref[s : s + 1, :]
-        for s in range(ROWS):
-            u = u_ref[s + 1]
-            laplace = u_ref[s] + u_ref[s + 2] + turn(u, 1) + turn(u, -1) - 4.0 * u
-            w_ref[s] = w_ref[s] + k_ref[s : s + 1, :] * laplace
-
-
-def spread_body(slot_ref, x_ref, out_ref, kept_ref, z_ref, w_ref, u_ref, table_ref):
+def sweep(load, k_ref, store):
+    before, here, conduct = None, load(0), k_ref[0:1, :]
+    u = here * conduct
+    for s in range(ROWS):
+        laplace = turn(u, 1) + turn(u, -1) - 4.0 * u
+        if before is not None:
+            laplace = laplace + before
+        if s + 1 < ROWS:
+            after, conduct_after = load(s + 1), k_ref[s + 1 : s + 2, :]
+            u_after = after * conduct_after
+            laplace = laplace + u_after
+        store(s, here + conduct * laplace)
+        if s + 1 < ROWS:
+            before, here, conduct, u = u, after, conduct_after, u_after
+
+
+def piece(value, q):
+    return value[:, q * LANES : (q + 1) * LANES]
+
+
+def spread_body(slot_ref, x_ref, out_ref, kept_ref, z_ref, w_ref, table_ref):
+    lane = lanes_of((8, LANES))
     z_ref[...] = x_ref[...].astype(F32)
     for q in range(PIECES):
         hi, lo = q, PIECES + q
@@ -178,30 +202,39 @@
             z_ref[pl.ds((hi // 2) * 8 + 6 + hi % 2, ROWS, stride=64), :]
             + z_ref[pl.ds((lo // 2) * 8 + 6 + lo % 2, ROWS, stride=64), :]
         )
-        for s in range(ROWS):
-            w_ref[s, :, q * LANES : (q + 1) * LANES] = z_ref[pl.ds(s * 64 + q, 8, stride=8), :]
-    diffuse_rows(w_ref, u_ref, kept_ref)
-    lane = lanes_of((8, LANES))
-    for s in range(ROWS):
+
+    def arrived(s):
+        return jnp.concatenate([z_ref[pl.ds(s * 64 + q, 8, stride=8), :] for q in range(PIECES)], axis=1)
+
+    def keep(s, value):
+        w_ref[s] = value
+
+    def cut(s, value):
         for c in range(COLS):
             parts = [
-                (low, high, turn(w_ref[s, :, a * LANES : (a + 1) * LANES], rotation))
-                for a, _, low, high, rotation in span(0, c * TC)
+                (low, high, turn(piece(value, a), rotation)) for a, _, low, high, rotation in span(0, c * TC)
             ]
             table_ref[c * ROWS + s] = chain(parts, lane)
+
+    sweep(arrived, kept_ref, keep)
+    sweep(lambda s: w_ref[s], kept_ref, keep)
+    for s in range(ROWS):
+        cut(s, w_ref[s])
     table_ref[BLANK] = jnp.zeros((8, LANES), F32)
 
-    def reader(s, carry):
-        runs = [[], [], []]
-        for j in range(NB):
-            tile = table_ref[slot_ref[s * NB + j]]
-            for _, b, low, high, rotation in span(j * TC, 0):
-                runs[b].append((low, high, turn(tile, rotation)))
-        for b in range(3):
-            out_ref[s, :, b * LANES : (b + 1) * LANES] = chain(runs[b], lane).astype(BF16)
-        return carry
-
-    lax.fori_loop(0, ROWS, reader, 0)
+    ahead = 2
+    waiting = {}
+    for s in range(ROWS + ahead):
+        if s < ROWS:
+            waiting[s] = [table_ref[slot_ref[s * NB + j]] for j in range(NB)]
+        if s >= ahead:
+            tiles = waiting.pop(s - ahead)
+            runs = [[], [], []]
+            for j in range(NB):
+                for _, b, low, high, rotation in span(j * TC, 0):
+                    runs[b].append((low, high, turn(tiles[j], rotation)))
+            for b in range(3):
+                out_ref[s - ahead, :, b * LANES : (b + 1) * LANES] = chain(runs[b], lane).astype(BF16)
 
 
 def observe_body(x_ref, f_ref, weight_ref, out_ref, x2_ref, g_ref):
@@ -237,23 +270,24 @@
     out_ref[TW:TWP] = jnp.zeros((TWP - TW, 8, NB * TC), BF16)
 
 
-def collect_body(slot_ref, x_ref, k_ref, out_ref, z_ref, w_ref, u_ref, table_ref):
+def collect_body(slot_ref, x_ref, k_ref, out_ref, z_ref, w_ref, table_ref):
     lane = lanes_of((8, LANES))
     table_ref[...] = jnp.zeros(table_ref.shape, F32)
 
     def reader(s, carry):
         value = x_ref[s].astype(F32)
+        tiles = [slot_ref[s * NB + j] for j in range(NB)]
+        sums = []
         for j in range(NB):
-            parts = [
-                (low, high, turn(value[:, a * LANES : (a + 1) * LANES], rotation))
-                for a, _, low, high, rotation in span(0, j * TC)
-            ]
-            g = slot_ref[s * NB + j]
-            table_ref[g] = table_ref[g] + chain(parts, lane)
+            parts = [(low, high, turn(piece(value, a), rotation)) for a, _, low, high, rotation in span(0, j * TC)]
+            sums.append(table_ref[tiles[j]] + chain(parts, lane))
+        for j in range(NB):
+            table_ref[tiles[j]] = sums[j]
         return carry
 
-    lax.fori_loop(0, ROWS, reader, 0)
-    for s in range(ROWS):
+    lax.fori_loop(0, ROWS, reader, 0, unroll=True)
+
+    def joined(s):
         runs = [[] for _ in range(PIECES)]
         for c in range(COLS):
             tile = table_ref[c * ROWS + s]
@@ -262,14 +296,21 @@
         runs[-1].append((TAIL, TAIL + 2, turn(table_ref[s], TAIL)))
         runs[-1].append((TAIL + 2, LANES - 2, jnp.zeros((8, LANES), F32)))
         runs[-1].append((LANES - 2, LANES, turn(table_ref[(COLS - 1) * ROWS + s], TAIL)))
-        for b in range(PIECES):
-            w_ref[s, :, b * LANES : (b + 1) * LANES] = chain(runs[b], lane)
-    diffuse_rows(w_ref, u_ref, k_ref)
+        return jnp.concatenate([chain(run, lane) for run in runs], axis=1)
+
+    def keep(s, value):
+        w_ref[s] = value
+
+    def leave(s, value):
+        for q in range(PIECES):
+            z_ref[pl.ds(s * 8 * PIECES + q, 8, stride=PIECES), :] = piece(value, q)
+
     for s in range(ROWS):
-        for q in range(PIECES):
-            z_ref[pl.ds(s * 64 + q, 8, stride=8), :] = w_ref[s, :, q * LANES : (q + 1) * LANES]
-        for q in range(PIECES, 8):
-            z_ref[pl.ds(s * 64 + q, 8, stride=8), :] = jnp.zeros((8, LANES), F32)
+        keep(s, joined(s))
+    for _ in range(DIFF):
+        sweep(lambda s: w_ref[s], k_ref, keep)
+    for s in range(ROWS):
+        leave(s, w_ref[s])
     out_ref[...] = z_ref[...].astype(BF16)
 
 
@@ -278,7 +319,7 @@
     for w in range(NW):
         for q in range(PIECES):
             w_ref[TWP * w : TWP * (w + 1), q * LANES : (q + 1) * LANES] = z_ref[
-                pl.ds(w * 8 + q, TWP, stride=64), :
+                pl.ds(w * PIECES + q, TWP, stride=NW * PIECES), :
             ].astype(BF16)
     x = w_ref[...]
     down = (((0,), (0,)), ((), ()))
@@ -314,7 +355,7 @@
     sums_ref[...] = jnp.broadcast_to(line, sums_ref.shape)
 
 
-def update_body(sums_ref, it_ref, r_ref, d_ref, image_ref, it_out, r_out, d_out):
+def update_body(sums_ref, it_ref, r_ref, d_ref, image_ref, it_out, r_out, d_out, it_new, r_new, d_new, sem):
     line = jnp.sum(sums_ref[...], axis=0, keepdims=True)
     lane = lanes_of((8, LANES))
     k = lax.broadcasted_iota(jnp.int32, (8, LANES), 0)
@@ -324,12 +365,22 @@
     step = rr / dq
     norm = jnp.maximum(rr + step * (step * qq - 2.0 * rq), 0.0)
     ratio = norm / rr
-    for t in range(TW):
-        d = d_ref[t]
-        after = r_ref[t] - step * image_ref[t]
-        it_out[t] = it_ref[t] + step * d
-        r_out[t] = after
-        d_out[t] = after + ratio * d
+    count = 5
+    rows = TW // count
+    copies = []
+    for i in range(count):
+        for t in range(i * rows, (i + 1) * rows):
+            d = d_ref[t]
+            after = r_ref[t] - step * image_ref[t]
+            it_new[t] = it_ref[t] + step * d
+            r_new[t] = after
+            d_new[t] = after + ratio * d
+        at = pl.ds(i * rows, rows)
+        for n, (new, out) in enumerate(((it_new, it_out), (r_new, r_out), (d_new, d_out))):
+            copies.append(pltpu.make_async_copy(new.at[at], out.at[at], sem.at[n, i]))
+            copies[-1].start()
+    for copy in copies:
+        copy.wait()
 
 
 def shape(dims, dtype):
@@ -345,18 +396,29 @@
     ]
     grid = (ROWS, 8, WIDE)
     with jax.named_scope("prepare"):
-        message, hi, lo = call(
+        message = call(
             prepare_body,
-            (shape((8, TWP, WIDE), BF16), shape((256, 256), BF16), shape((256, 256), BF16)),
+            shape((8, TWP, WIDE), BF16),
             [
                 pltpu.VMEM((PIECES, 256, LANES), F32),
-                pltpu.VMEM((240, 256), F32),
-                pltpu.VMEM((256, 256), F32),
+                pltpu.VMEM((240, LON), F32),
                 pltpu.VMEM((240, LANES), F32),
+                pltpu.SMEM((1, NB), jnp.int32),
+                pltpu.SemaphoreType.DMA((6,)),
+                pltpu.SemaphoreType.DMA,
             ],
-            1,
-        )(block_tile, direction.reshape(240, LON), temporal_factor)
+            "hh",
+        )(
+            pltpu.with_memory_space_constraint(block_tile, pltpu.HBM),
+            pltpu.with_memory_space_constraint(direction.reshape(240, LON), pltpu.HBM),
+        )
         message = lax.all_to_all(message, "tm", 0, 0, tiled=True)
+    with jax.named_scope("factor"):
+        hi, lo = call(
+            factor_body,
+            (shape((256, 256), BF16), shape((256, 256), BF16)),
+            [pltpu.VMEM((240, 256), F32), pltpu.VMEM((256, 256), F32)],
+        )(temporal_factor)
     with jax.named_scope("mix"):
         message = call(
             mix_body,
@@ -374,10 +436,9 @@
             [
                 pltpu.VMEM((2048, LANES), F32),
                 pltpu.VMEM(grid, F32),
-                pltpu.VMEM((ROWS + 2, 8, WIDE), F32),
                 pltpu.VMEM((BLANK + 1, 8, LANES), F32),
             ],
-            1,
+            "s",
         )(slots, message.reshape(2048, LANES))
         message = lax.all_to_all(message, "space", 0, 0, tiled=True)
     with jax.named_scope("observe"):
@@ -390,22 +451,21 @@
     with jax.named_scope("collect"):
         message = call(
             collect_body,
-            shape((2048, LANES), BF16),
+            shape((1536, LANES), BF16),
             [
-                pltpu.VMEM((2048, LANES), F32),
+                pltpu.VMEM((1536, LANES), F32),
                 pltpu.VMEM(grid, F32),
-                pltpu.VMEM((ROWS + 2, 8, WIDE), F32),
                 pltpu.VMEM((BLANK + 1, 8, LANES), F32),
             ],
-            1,
+            "s",
         )(slots, message, conduct)
-        message = lax.all_to_all(message.reshape(256, 8, LANES), both, 0, 0, tiled=True)
+        message = lax.all_to_all(message.reshape(768, 2, LANES), both, 0, 0, tiled=True)
     with jax.named_scope("unmix"):
         message = call(
             unmix_body,
             shape((256, WIDE), BF16),
-            [pltpu.VMEM((2048, LANES), F32), pltpu.VMEM((256, WIDE), BF16)],
-        )(message.reshape(2048, LANES), hi, lo)
+            [pltpu.VMEM((1536, LANES), F32), pltpu.VMEM((256, WIDE), BF16)],
+        )(message.reshape(1536, LANES), hi, lo)
         message = lax.all_to_all(message.reshape(8, TWP, WIDE), "tm", 0, 0, tiled=True)
     with jax.named_scope("image"):
         image, sums = call(
@@ -415,9 +475,13 @@
         )(message.reshape(256, WIDE), direction, residual)
         sums = lax.all_to_all(sums, both, 0, 0, tiled=True)
     with jax.named_scope("update"):
-        outs = call(update_body, tuple(shape((TW, 8, LON), F32) for _ in range(3)))(
-            sums, iterate, residual, direction, image
-        )
+        whole = (TW, 8, LON)
+        outs = call(
+            update_body,
+            tuple(shape(whole, F32) for _ in range(3)),
+            [pltpu.VMEM(whole, F32) for _ in range(3)] + [pltpu.SemaphoreType.DMA((3, 5))],
+            out_places="hhh",
+        )(sums, iterate, residual, direction, image)
     return tuple(jnp.transpose(value, (1, 0, 2)) for value in outs)
 
 

time: 156 us -> 146 us (0.936)
  Pallas kernels: 17.2 us -> 13.3 us
  blocking collectives: 120 us -> 117 us
  local copies, waits for them, and re-layouts: 2.83 us -> 0.12 us
    all_to_all x2 -> x1, blocking collectives: 60.1 us -> 32.1 us  [local(): lax.all_to_all(message.reshape(256, 8, LANES), both, 0, 0, tiled=True)]
    all_to_all x0 -> x1, blocking collectives: none -> 25.1 us  [local(): lax.all_to_all(message.reshape(768, 2, LANES), both, 0, 0, tiled=True)]
    pallas_call x8 -> x9, Pallas kernels: 17.2 us -> 13.3 us  [run(): pl.pallas_call(body, out_shape=outs, in_specs=[pl.BlockSpec(memory_space=...]
    unnamed x18 -> x14, local copies, waits for them, and re-layouts: 2.74 us -> 0.03 us
where the time goes in v2:
time: 146 us; the launch traced here: 145 us
  blocking collectives  117 us (80%)
  Pallas kernels  13.3 us (9%)
  waiting for transfers between devices  7.44 us (5%)
  starting transfers between devices  6.61 us (5%)
    all_to_all x1, blocking collectives, local(): lax.all_to_all(message.reshape(256, 8, LANES), both, 0, 0, tiled=True)  32.1 us
    all_to_all x2, blocking collectives, local(): message = lax.all_to_all(message, 'space', 0, 0, tiled=True)  28.4 us
    all_to_all x1, blocking collectives, local(): lax.all_to_all(message.reshape(768, 2, LANES), both, 0, 0, tiled=True)  25.1 us
    all_to_all x1, blocking collectives, local(): sums = lax.all_to_all(sums, both, 0, 0, tiled=True)  18.7 us
    pallas_call x9, Pallas kernels, run(): pl.pallas_call(body, out_shape=outs, in_specs=[pl.BlockSpec(memory_space=...  13.3 us
    all_to_all x1, blocking collectives, local(): lax.all_to_all(message.reshape(8, TWP, WIDE), 'tm', 0, 0, tiled=True)  12.6 us
    all_to_all x1, waiting for transfers between devices, local(): message = lax.all_to_all(message, 'tm', 0, 0, tiled=True)  7.44 us
    all_to_all x1, starting transfers between devices, local(): message = lax.all_to_all(message, 'tm', 0, 0, tiled=True)  6.61 us
  transfers between devices with their start and end apart: 1, of which 1 were waited for; matrix products, arithmetic and copies ran while one was open for 0% of the time, Pallas kernels for 0%

profile of v2, /device:TPU:1, one launch (start us, length us, event | category | flops | bytes accessed | tf_op | source)
XLA Modules:
  0.0 145.3 jit_solution(14638408332431660933)
XLA Ops:
  0.6 0.0 copy-start.6
  0.6 0.0 copy-start.4
  0.7 2.5 %prepare.1 = bf16[8,32,768]{2,1,0:T(8,128)(2,1)} custom-call(s32[1,8]{1,0:T(1,128)} %tile_hbm.1, f32[240,720]{1,0:T(8,128)} %bitcast.23), custom_call_target="tpu_custom_call" | custom-call | tf_op jit(solution)/shard_map/prepare/pallas_call | solution.py:35
  3.1 6.6 %all-to-all-start = ((bf16[8,32,768]{2,1,0:T(8,128)(2,1)}), bf16[8,32,768]{2,1,0:T(8,128)(2,1)S(1)}, u32[]{:S(2)}, u32[]{:S(2)}) async-start(bf16[8,32,768]{2,1,0:T(8,128)(2,1)} %prepare.1), calls=%async_computation | async-start | bytes 786432 | tf_op jit(solution)/shard_map/prepare/all_to_all | solution.py:415
  9.7 0.0 copy-done.6
  9.7 0.0 copy-done.4
  9.7 0.6 factor.1
  10.4 7.4 %all-to-all-done = bf16[8,32,768]{2,1,0:T(8,128)(2,1)S(1)} async-done(((bf16[8,32,768]{2,1,0:T(8,128)(2,1)}), bf16[8,32,768]{2,1,0:T(8,128)(2,1)S(1)}, u32[]{:S(2)}, u32[]{:S(2)}) %all-to-all-start) | async-done | bytes 393248 | tf_op jit(solution)/shard_map/prepare/all_to_all | solution.py:415
  17.8 0.0 copy-start.2
  17.8 0.0 copy-start.5
  17.8 0.9 mix.1
  18.7 32.1 %all_to_all.41 = bf16[256,8,128]{2,1,0:T(8,128)(2,1)S(1)} all-to-all(bf16[256,8,128]{2,1,0:T(8,128)(2,1)S(1)} %bitcast.30), channel_id=1, replica_groups=mesh['space'=32,'tm'=8] {'space','tm'}, dimensions={0} | all-to-all | bytes 1048576 | tf_op jit(solution)/shard_map/mix/all_to_all | solution.py:428
  50.8 0.1 slice_convert_fusion
  50.9 0.1 fusion
  51.0 0.1 reshape.48.slot_ref
  51.1 2.4 %spread.1 = (bf16[32,8,384]{2,1,0:T(8,128)(2,1)S(1)}, f32[32,768]{1,0:T(8,128)S(1)}) custom-call(s32[256]{0:T(256)S(1)} %reshape.48.slot_ref, bf16[2048,128]{1,0:T(8,128)(2,1)S(1)} %bitcast.29), custom_call_target="tpu_custom_call" | custom-call | tf_op jit(solution)/shard_map/spread/pallas_call | solution.py:35
  53.5 14.1 %all_to_all.42.x_ref = bf16[32,8,384]{2,1,0:T(8,128)(2,1)S(1)} all-to-all(bf16[32,8,384]{2,1,0:T(8,128)(2,1)S(1)} %get-tuple-element.14), channel_id=1, replica_groups=mesh['space'=32,'tm'=8] {'space'}, dimensions={0} | all-to-all | bytes 393216 | tf_op jit(solution)/shard_map/spread/all_to_all | solution.py:443
  67.6 0.0 copy-done.2
  67.6 0.0 copy-done.5
  67.6 1.4 observe.1
  69.0 14.3 %all_to_all.43.x_ref = bf16[32,8,384]{2,1,0:T(8,128)(2,1)S(1)} all-to-all(bf16[32,8,384]{2,1,0:T(8,128)(2,1)S(1)} %observe.1), channel_id=1, replica_groups=mesh['space'=32,'tm'=8] {'space'}, dimensions={0} | all-to-all | bytes 393216 | tf_op jit(solution)/shard_map/observe/all_to_all | solution.py:450
  83.3 0.0 copy-start
  83.3 0.0 copy-start.1
  83.3 2.6 %collect.1 = bf16[1536,128]{1,0:T(8,128)(2,1)S(1)} custom-call(s32[256]{0:T(256)S(1)} %reshape.48.slot_ref, bf16[32,8,384]{2,1,0:T(8,128)(2,1)S(1)} %all_to_all.43.x_ref, f32[32,768]{1,0:T(8,128)S(1)} %get-tuple-element.15.k_ref), custom_call_target="tpu_custom_call" | custom-call | tf_op jit(solution)/shard_map/collect/pallas_call | solution.py:35
  86.0 25.1 %all_to_all.44 = bf16[768,2,128]{2,1,0:T(2,128)(2,1)S(1)} all-to-all(bf16[768,2,128]{2,1,0:T(2,128)(2,1)S(1)} %bitcast.34), channel_id=1, replica_groups=mesh['space'=32,'tm'=8] {'space','tm'}, dimensions={0} | all-to-all | bytes 786432 | tf_op jit(solution)/shard_map/collect/all_to_all | solution.py:462
  111.0 0.6 unmix.1
  111.7 0.0 copy-start.3
  111.7 12.6 %all_to_all.45 = bf16[8,32,768]{2,1,0:T(8,128)(2,1)S(1)} all-to-all(bf16[8,32,768]{2,1,0:T(8,128)(2,1)S(1)} %bitcast.36), channel_id=1, replica_groups=mesh['space'=32,'tm'=8] {'tm'}, dimensions={0} | all-to-all | bytes 786432 | tf_op jit(solution)/shard_map/unmix/all_to_all | solution.py:469
  124.3 0.0 copy-done
  124.3 0.0 copy-done.1
  124.3 0.7 image.1
  125.0 18.7 %all_to_all.46 = f32[256,1,128]{2,1,0:T(1,128)S(1)} all-to-all(f32[256,1,128]{2,1,0:T(1,128)S(1)} %bitcast.39), channel_id=1, replica_groups=mesh['space'=32,'tm'=8] {'space','tm'}, dimensions={0} | all-to-all | bytes 262144 | tf_op jit(solution)/shard_map/image/all_to_all | solution.py:476
  143.7 0.0 copy-done.3
  143.7 1.6 %update.1 = (f32[30,8,720]{2,1,0:T(8,128)}, f32[30,8,720]{2,1,0:T(8,128)}, f32[30,8,720]{2,1,0:T(8,128)}) custom-call(f32[256,128]{1,0:T(8,128)S(1)} %bitcast.38, f32[30,8,720]{2,1,0:T(8,128)S(1)} %bitcast.37, f32[30,8,720]{2,1,0:T(8,128)S(1)} %bitcast.27, f32[30,8,720]{2,1,0:T(8,128)S(1)} %bitcast.25, f32[30,8,720]{2,1,0:T(8,128)S(1)} %get-tuple-element.17.image_ref), custom_call_target="tpu_custom_call" | custom-call | tf_op jit(solution)/shard_map/update/pallas_call | solution.py:35
  (1 shorter events, 0.0 us)
Async XLA Ops:
  0.6 9.1 %copy-start.6 = (f32[720]{0:T(1024)S(1)}, f32[720]{0:T(1024)}, u32[]{:S(2)}) copy-start(f32[720]{0:T(1024)} %param.11) | copy-start | bytes 8644
  0.6 9.1 %copy-start.4 = (f32[240,240]{1,0:T(8,128)S(1)}, f32[240,240]{1,0:T(8,128)}, u32[]{:S(2)}) copy-start(f32[240,240]{1,0:T(8,128)} %factor_ref.1) | copy-start | bytes 691204
  3.1 14.7 %all-to-all-start = ((bf16[8,32,768]{2,1,0:T(8,128)(2,1)}), bf16[8,32,768]{2,1,0:T(8,128)(2,1)S(1)}, u32[]{:S(2)}, u32[]{:S(2)}) async-start(bf16[8,32,768]{2,1,0:T(8,128)(2,1)} %prepare.1), calls=%async_computation | async-start | bytes 786432 | tf_op jit(solution)/shard_map/prepare/all_to_all | solution.py:415
  17.8 49.8 %copy-start.2 = (bf16[1,8,64,1440]{3,2,1,0:T(8,128)(2,1)S(1)}, bf16[1,8,64,1440]{3,2,1,0:T(8,128)(2,1)}, u32[]{:S(2)}) copy-start(bf16[1,8,64,1440]{3,2,1,0:T(8,128)(2,1)} %param.14) | copy-start | bytes 4423684
  17.8 49.8 %copy-start.5 = (f32[1,1,64]{2,1,0:T(1,128)S(1)}, f32[1,1,64]{2,1,0:T(1,128)}, u32[]{:S(2)}) copy-start(f32[1,1,64]{2,1,0:T(1,128)} %param.15) | copy-start | bytes 772
  83.3 41.0 %copy-start = (f32[8,30,720]{2,0,1:T(8,128)S(1)}, f32[8,30,720]{2,0,1:T(8,128)}, u32[]{:S(2)}) copy-start(f32[8,30,720]{2,0,1:T(8,128)} %param.10) | copy-start | bytes 2073604
  83.3 41.0 %copy-start.1 = (f32[8,30,720]{2,0,1:T(8,128)S(1)}, f32[8,30,720]{2,0,1:T(8,128)}, u32[]{:S(2)}) copy-start(f32[8,30,720]{2,0,1:T(8,128)} %param.9) | copy-start | bytes 2073604
  111.7 32.0 %copy-start.3 = (f32[8,30,720]{2,0,1:T(8,128)S(1)}, f32[8,30,720]{2,0,1:T(8,128)}, u32[]{:S(2)}) copy-start(f32[8,30,720]{2,0,1:T(8,128)} %param.8) | copy-start | bytes 2073604

commit v3 on v2

--- a/solution.py
+++ b/solution.py
@@ -73,34 +73,63 @@
     return result
 
 
-def prepare_body(tile_hbm, d_hbm, out_ref, z_ref, d_ref, tail_ref, tile_ref, sem, tile_sem):
-    count = 6
-    rows = 240 // count
+def wrapped(first, tail, lane):
+    return jnp.where(
+        lane < TAIL,
+        tail,
+        jnp.where(lane < TAIL + 2, turn(first, TAIL), jnp.where(lane >= LANES - 2, turn(tail, TC), 0.0)),
+    )
+
+
+def prepare_body(
+    tile_hbm, d_hbm, factor_hbm, conduct_hbm, out_ref, hi_ref, lo_ref, cut_ref,
+    z_ref, tail_ref, wide_tail_ref, tile_ref, factor_ref, wide_ref, deep_ref, conduct_ref, row_ref, sem, more_sem,
+):
+    factor_copy = pltpu.make_async_copy(factor_hbm, factor_ref, more_sem.at[0])
+    tile_copy = pltpu.make_async_copy(tile_hbm, tile_ref, more_sem.at[1])
+    conduct_copy = pltpu.make_async_copy(conduct_hbm, conduct_ref, more_sem.at[2])
+    last = PIECES - 1
     copies = [
-        pltpu.make_async_copy(d_hbm.at[pl.ds(i * rows, rows)], d_ref.at[pl.ds(i * rows, rows)], sem.at[i])
-        for i in range(count)
-    ]
-    tile_copy = pltpu.make_async_copy(tile_hbm, tile_ref, tile_sem)
+        pltpu.make_async_copy(
+            d_hbm.at[:, pl.ds(q * LANES, LANES)], z_ref.at[q, pl.ds(0, 240), :], sem.at[q]
+        )
+        for q in range(last)
+    ] + [pltpu.make_async_copy(d_hbm.at[:, pl.ds(last * LANES, TAIL)], tail_ref, sem.at[last])]
+    factor_copy.start()
     for copy in copies:
         copy.start()
     tile_copy.start()
-    lane = lanes_of((rows, LANES))
+    conduct_copy.start()
     for q in range(PIECES - 1):
         z_ref[q, 240:256, :] = jnp.zeros((16, LANES), F32)
     z_ref[PIECES - 1, 248:256, :] = jnp.zeros((8, LANES), F32)
-    for i in range(count):
-        copies[i].wait()
-        at = pl.ds(i * rows, rows)
-        tail_ref[at, 0:TAIL] = d_ref[at, (PIECES - 1) * LANES : LON]
-        for q in range(PIECES - 1):
-            z_ref[q, at, :] = d_ref[at, q * LANES : (q + 1) * LANES]
-        tail = tail_ref[at, :]
-        first = d_ref[at, 0:LANES]
-        z_ref[PIECES - 1, at, :] = jnp.where(
-            lane < TAIL,
-            tail,
-            jnp.where(lane < TAIL + 2, turn(first, TAIL), jnp.where(lane >= LANES - 2, turn(tail, TC), 0.0)),
-        )
+    deep_ref[...] = jnp.zeros((256, 256), F32)
+    wide_ref[:, LANES:] = jnp.zeros((240, LANES), F32)
+    factor_copy.wait()
+    wide_ref[:, 0:240] = factor_ref[...]
+    factor = wide_ref[...]
+    line = lanes_of((240, LANES))
+    runs = [[], []]
+    for w in range(NW):
+        for a, b, low, high, rotation in span(TWP * w, TW * w, TW):
+            runs[b].append((low, high, turn(piece(factor, a), rotation)))
+        low = TWP * w % LANES + TW
+        runs[TWP * w // LANES].append((low, low + TWP - TW, jnp.zeros((240, LANES), F32)))
+    for b in range(2):
+        wide_ref[:, b * LANES : (b + 1) * LANES] = chain(runs[b], line)
+    for w in range(NW):
+        deep_ref[TWP * w : TWP * w + TW, :] = wide_ref[TW * w : TW * w + TW, :]
+    row = lax.broadcasted_iota(jnp.int32, (256, 256), 0)
+    column = lanes_of((256, 256))
+    codes_here = ((column & 31) == TW) & ((row >> 5) == (column >> 5)) & ((row & 31) < TW)
+    full = jnp.where(codes_here, 1.0, deep_ref[...])
+    hi = full.astype(BF16)
+    hi_ref[...] = hi
+    lo_ref[...] = (full - hi.astype(F32)).astype(BF16)
+    copies[last].wait()
+    copies[0].wait()
+    wide_tail_ref[:, 0:TAIL] = tail_ref[...]
+    z_ref[last, 0:240, :] = wrapped(z_ref[0, 0:240, :], wide_tail_ref[...], lanes_of((240, LANES)))
     tile_copy.wait()
     line = lanes_of((8, LANES))
     codes = jnp.zeros((8, LANES), F32)
@@ -115,62 +144,39 @@
         codes = jnp.where(line == IDX + j, row, codes)
         codes = jnp.where(line == IDX + NB + j, col, codes)
     z_ref[PIECES - 1, 240:248, :] = codes
+    conduct_copy.wait()
+    lane = lanes_of((1, LANES))
+    row_ref[...] = jnp.zeros((8, LANES), F32)
+    row_ref[0:1, 0:TAIL] = conduct_ref[pl.ds((PIECES - 1) * LANES, TAIL)].reshape(1, TAIL)
+    cut_ref[...] = jnp.zeros((16, LANES), F32)
     for q in range(PIECES):
+        if q < PIECES - 1:
+            part = conduct_ref[pl.ds(q * LANES, LANES)].reshape(1, LANES)
+        else:
+            part = wrapped(conduct_ref[pl.ds(0, LANES)].reshape(1, LANES), row_ref[0:1, :], lane)
+        hi = part.astype(BF16).astype(F32)
+        cut_ref[q : q + 1, :] = hi
+        cut_ref[PIECES + q : PIECES + q + 1, :] = part - hi
+    for q in range(PIECES):
+        if 0 < q < last:
+            copies[q].wait()
         for k in range(8):
             out_ref[k, :, q * LANES : (q + 1) * LANES] = z_ref.at[q][pl.ds(k, TWP, stride=8), :].astype(BF16)
 
 
-def factor_body(factor_ref, hi_ref, lo_ref, wide_ref, deep_ref):
-    wide_ref[:, LANES:] = jnp.zeros((240, LANES), F32)
-    wide_ref[:, 0:240] = factor_ref[...]
-    factor = wide_ref[...]
-    column = lanes_of((240, 256))
-    padded = jnp.zeros((240, 256), F32)
-    for w in range(NW):
-        here = ((column >> 5) == w) & ((column & 31) < TW)
-        padded = jnp.where(here, turn(factor, 2 * w), padded)
-    wide_ref[...] = padded
-    deep_ref[...] = jnp.zeros((256, 256), F32)
-    for w in range(NW):
-        deep_ref[TWP * w : TWP * w + TW, :] = wide_ref[TW * w : TW * w + TW, :]
-    rows = lax.broadcasted_iota(jnp.int32, (256, 256), 0)
-    column = lanes_of((256, 256))
-    codes_here = ((column & 31) == TW) & ((rows >> 5) == (column >> 5)) & ((rows & 31) < TW)
-    full = jnp.where(codes_here, 1.0, deep_ref[...])
-    hi = full.astype(BF16)
-    hi_ref[...] = hi
-    lo_ref[...] = (full - hi.astype(F32)).astype(BF16)
-
-
-def mix_body(x_ref, hi_ref, lo_ref, conduct_ref, out_ref, z_ref, k_ref, row_ref):
+def mix_body(x_ref, hi_ref, lo_ref, cut_ref, out_ref, z_ref):
     x = x_ref[...]
     mixed = jnp.dot(hi_ref[...], x, preferred_element_type=F32) + jnp.dot(
         lo_ref[...], x, preferred_element_type=F32
     )
+    m = lax.axis_index("tm")
+    for e in range(2):
+        part = cut_ref[pl.ds(2 * m + e, 1), :]
+        z_ref[pl.ds(PIECES + e, 256, stride=8), :] = jnp.broadcast_to(part, (256, LANES))
     for w in range(NW):
         for q in range(PIECES):
             z_ref[pl.ds(w * 8 + q, TWP, stride=64), :] = mixed[TWP * w : TWP * (w + 1), q * LANES : (q + 1) * LANES]
-    lane = lanes_of((1, LANES))
-    row_ref[...] = jnp.zeros((8, LANES), F32)
-    row_ref[0:1, 0:TAIL] = conduct_ref[0:1, (PIECES - 1) * LANES : LON]
-    tail = row_ref[0:1, :]
-    first = conduct_ref[0:1, 0:LANES]
-    last = jnp.where(
-        lane < TAIL,
-        tail,
-        jnp.where(lane < TAIL + 2, turn(first, TAIL), jnp.where(lane >= LANES - 2, turn(tail, TC), 0.0)),
-    )
-    k_ref[...] = jnp.zeros((16, LANES), F32)
-    for q in range(PIECES):
-        part = last if q == PIECES - 1 else conduct_ref[0:1, q * LANES : (q + 1) * LANES]
-        hi = part.astype(BF16).astype(F32)
-        k_ref[q : q + 1, :] = hi
-        k_ref[PIECES + q : PIECES + q + 1, :] = part - hi
-    m = lax.axis_index("tm")
-    for e in range(2):
-        part = k_ref[pl.ds(2 * m + e, 1), :]
-        z_ref[pl.ds(6 + e, 256, stride=8), :] = jnp.broadcast_to(part, (256, LANES))
-    out_ref[...] = z_ref[...].astype(BF16)
+    out_ref[...] = z_ref[0:2048, :].astype(BF16)
 
 
 def sweep(load, k_ref, store):
@@ -193,9 +199,15 @@
     return value[:, q * LANES : (q + 1) * LANES]
 
 
-def spread_body(slot_ref, x_ref, out_ref, kept_ref, z_ref, w_ref, table_ref):
+def spread_body(x_ref, out_ref, kept_ref, code_ref, z_ref, w_ref, table_ref, slot_ref, sem):
     lane = lanes_of((8, LANES))
-    z_ref[...] = x_ref[...].astype(F32)
+    z_ref[0:2048, :] = x_ref[...].astype(F32)
+    codes = z_ref[pl.ds(PIECES - 1, ROWS, stride=64), :]
+    line = lanes_of((ROWS, LANES))
+    codes = jnp.where((line >= IDX) & (line < IDX + NB), turn(codes, -NB) * ROWS + codes, 0.0)
+    code_ref[...] = codes.astype(jnp.int32)
+    slot_copy = pltpu.make_async_copy(code_ref, slot_ref, sem)
+    slot_copy.start()
     for q in range(PIECES):
         hi, lo = q, PIECES + q
         kept_ref[:, q * LANES : (q + 1) * LANES] = (
@@ -222,11 +234,12 @@
         cut(s, w_ref[s])
     table_ref[BLANK] = jnp.zeros((8, LANES), F32)
 
+    slot_copy.wait()
     ahead = 2
     waiting = {}
     for s in range(ROWS + ahead):
         if s < ROWS:
-            waiting[s] = [table_ref[slot_ref[s * NB + j]] for j in range(NB)]
+            waiting[s] = [table_ref[slot_ref[s, IDX + j]] for j in range(NB)]
         if s >= ahead:
             tiles = waiting.pop(s - ahead)
             runs = [[], [], []]
@@ -270,13 +283,16 @@
     out_ref[TW:TWP] = jnp.zeros((TWP - TW, 8, NB * TC), BF16)
 
 
-def collect_body(slot_ref, x_ref, k_ref, out_ref, z_ref, w_ref, table_ref):
+def collect_body(slot_any, x_ref, k_ref, out_ref, z_ref, w_ref, table_ref, slot_ref, sem):
+    slot_copy = pltpu.make_async_copy(slot_any, slot_ref, sem)
+    slot_copy.start()
     lane = lanes_of((8, LANES))
     table_ref[...] = jnp.zeros(table_ref.shape, F32)
+    slot_copy.wait()
 
     def reader(s, carry):
         value = x_ref[s].astype(F32)
-        tiles = [slot_ref[s * NB + j] for j in range(NB)]
+        tiles = [slot_ref[s, IDX + j] for j in range(NB)]
         sums = []
         for j in range(NB):
             parts = [(low, high, turn(piece(value, a), rotation)) for a, _, low, high, rotation in span(0, j * TC)]
@@ -311,11 +327,11 @@
         sweep(lambda s: w_ref[s], k_ref, keep)
     for s in range(ROWS):
         leave(s, w_ref[s])
-    out_ref[...] = z_ref[...].astype(BF16)
+    out_ref[...] = z_ref[0:1536, :].astype(BF16)
 
 
 def unmix_body(x_ref, hi_ref, lo_ref, out_ref, z_ref, w_ref):
-    z_ref[...] = x_ref[...].astype(F32)
+    z_ref[0:1536, :] = x_ref[...].astype(F32)
     for w in range(NW):
         for q in range(PIECES):
             w_ref[TWP * w : TWP * (w + 1), q * LANES : (q + 1) * LANES] = z_ref[
@@ -331,7 +347,7 @@
 
 def image_body(x_ref, d_ref, r_ref, image_ref, sums_ref, z_ref):
     for q in range(PIECES):
-        z_ref[q] = x_ref[:, q * LANES : (q + 1) * LANES].astype(F32)
+        z_ref[q, 0:256, :] = x_ref[:, q * LANES : (q + 1) * LANES].astype(F32)
     totals = [jnp.zeros((8, 1), F32) for _ in range(4)]
     for q in range(PIECES):
         width = TAIL if q == PIECES - 1 else LANES
@@ -365,7 +381,7 @@
     step = rr / dq
     norm = jnp.maximum(rr + step * (step * qq - 2.0 * rq), 0.0)
     ratio = norm / rr
-    count = 5
+    count = 3
     rows = TW // count
     copies = []
     for i in range(count):
@@ -396,50 +412,52 @@
     ]
     grid = (ROWS, 8, WIDE)
     with jax.named_scope("prepare"):
-        message = call(
+        message, hi, lo, cut = call(
             prepare_body,
-            shape((8, TWP, WIDE), BF16),
+            (
+                shape((8, TWP, WIDE), BF16),
+                shape((256, 256), BF16),
+                shape((256, 256), BF16),
+                shape((16, LANES), F32),
+            ),
             [
-                pltpu.VMEM((PIECES, 256, LANES), F32),
-                pltpu.VMEM((240, LON), F32),
+                pltpu.VMEM((PIECES, 264, LANES), F32),
+                pltpu.VMEM((240, TAIL), F32),
                 pltpu.VMEM((240, LANES), F32),
                 pltpu.SMEM((1, NB), jnp.int32),
+                pltpu.VMEM((240, 240), F32),
+                pltpu.VMEM((240, 256), F32),
+                pltpu.VMEM((256, 256), F32),
+                pltpu.VMEM((LON,), F32),
+                pltpu.VMEM((8, LANES), F32),
                 pltpu.SemaphoreType.DMA((6,)),
+                pltpu.SemaphoreType.DMA((3,)),
+            ],
+            "hhhh",
+        )(
+            *[
+                pltpu.with_memory_space_constraint(value, pltpu.HBM)
+                for value in (block_tile, direction.reshape(240, LON), temporal_factor, diffusivity)
+            ]
+        )
+        message = lax.all_to_all(message, "tm", 0, 0, tiled=True)
+    with jax.named_scope("mix"):
+        message = call(mix_body, shape((2048, LANES), BF16), [pltpu.VMEM((2112, LANES), F32)])(
+            message.reshape(256, WIDE), hi, lo, cut
+        )
+        message = lax.all_to_all(message.reshape(256, 8, LANES), both, 0, 0, tiled=True)
+    with jax.named_scope("spread"):
+        message, conduct, slots = call(
+            spread_body,
+            (shape((ROWS, 8, NB * TC), BF16), shape((ROWS, WIDE), F32), shape((ROWS, LANES), jnp.int32)),
+            [
+                pltpu.VMEM((2112, LANES), F32),
+                pltpu.VMEM(grid, F32),
+                pltpu.VMEM((BLANK + 1, 8, LANES), F32),
+                pltpu.SMEM((ROWS, LANES), jnp.int32),
                 pltpu.SemaphoreType.DMA,
             ],
-            "hh",
-        )(
-            pltpu.with_memory_space_constraint(block_tile, pltpu.HBM),
-            pltpu.with_memory_space_constraint(direction.reshape(240, LON), pltpu.HBM),
-        )
-        message = lax.all_to_all(message, "tm", 0, 0, tiled=True)
-    with jax.named_scope("factor"):
-        hi, lo = call(
-            factor_body,
-            (shape((256, 256), BF16), shape((256, 256), BF16)),
-            [pltpu.VMEM((240, 256), F32), pltpu.VMEM((256, 256), F32)],
-        )(temporal_factor)
-    with jax.named_scope("mix"):
-        message = call(
-            mix_body,
-            shape((2048, LANES), BF16),
-            [pltpu.VMEM((2048, LANES), F32), pltpu.VMEM((16, LANES), F32), pltpu.VMEM((8, LANES), F32)],
-        )(message.reshape(256, WIDE), hi, lo, diffusivity.reshape(1, LON))
-        message = lax.all_to_all(message.reshape(256, 8, LANES), both, 0, 0, tiled=True)
-    with jax.named_scope("slots"):
-        codes = message.reshape(ROWS, 8, 8, LANES)[:, 0, PIECES - 1, IDX : IDX + 2 * NB].astype(F32)
-        slots = (codes[:, NB:] * ROWS + codes[:, :NB]).astype(jnp.int32).reshape(ROWS * NB)
-    with jax.named_scope("spread"):
-        message, conduct = call(
-            spread_body,
-            (shape((ROWS, 8, NB * TC), BF16), shape((ROWS, WIDE), F32)),
-            [
-                pltpu.VMEM((2048, LANES), F32),
-                pltpu.VMEM(grid, F32),
-                pltpu.VMEM((BLANK + 1, 8, LANES), F32),
-            ],
-            "s",
-        )(slots, message.reshape(2048, LANES))
+        )(message.reshape(2048, LANES))
         message = lax.all_to_all(message, "space", 0, 0, tiled=True)
     with jax.named_scope("observe"):
         message = call(
@@ -453,25 +471,27 @@
             collect_body,
             shape((1536, LANES), BF16),
             [
-                pltpu.VMEM((1536, LANES), F32),
+                pltpu.VMEM((1584, LANES), F32),
                 pltpu.VMEM(grid, F32),
                 pltpu.VMEM((BLANK + 1, 8, LANES), F32),
+                pltpu.SMEM((ROWS, LANES), jnp.int32),
+                pltpu.SemaphoreType.DMA,
             ],
-            "s",
+            "h",
         )(slots, message, conduct)
         message = lax.all_to_all(message.reshape(768, 2, LANES), both, 0, 0, tiled=True)
     with jax.named_scope("unmix"):
         message = call(
             unmix_body,
             shape((256, WIDE), BF16),
-            [pltpu.VMEM((1536, LANES), F32), pltpu.VMEM((256, WIDE), BF16)],
+            [pltpu.VMEM((1584, LANES), F32), pltpu.VMEM((256, WIDE), BF16)],
         )(message.reshape(1536, LANES), hi, lo)
         message = lax.all_to_all(message.reshape(8, TWP, WIDE), "tm", 0, 0, tiled=True)
     with jax.named_scope("image"):
         image, sums = call(
             image_body,
             (shape((TW, 8, LON), F32), shape((256, LANES), F32)),
-            [pltpu.VMEM((PIECES, 256, LANES), F32)],
+            [pltpu.VMEM((PIECES, 288, LANES), F32)],
         )(message.reshape(256, WIDE), direction, residual)
         sums = lax.all_to_all(sums, both, 0, 0, tiled=True)
     with jax.named_scope("update"):
@@ -479,7 +499,7 @@
         outs = call(
             update_body,
             tuple(shape(whole, F32) for _ in range(3)),
-            [pltpu.VMEM(whole, F32) for _ in range(3)] + [pltpu.SemaphoreType.DMA((3, 5))],
+            [pltpu.VMEM(whole, F32) for _ in range(3)] + [pltpu.SemaphoreType.DMA((3, 3))],
             out_places="hhh",
         )(sums, iterate, residual, direction, image)
     return tuple(jnp.transpose(value, (1, 0, 2)) for value in outs)

time: 146 us -> 144 us (0.986)
  blocking collectives: 117 us -> 131 us
  waiting for transfers between devices: 7.44 us -> 0 us
  starting transfers between devices: 6.61 us -> 0 us
  Pallas kernels: 13.3 us -> 11.8 us
    all_to_all x0 -> x1, blocking collectives: none -> 13.9 us  [local(): message = lax.all_to_all(message, 'tm', 0, 0, tiled=True)]
    all_to_all x1 -> x0, waiting for transfers between devices: 7.44 us -> none  [local(): message = lax.all_to_all(message, 'tm', 0, 0, tiled=True)]
    all_to_all x1 -> x0, starting transfers between devices: 6.61 us -> none  [local(): message = lax.all_to_all(message, 'tm', 0, 0, tiled=True)]
    pallas_call x9 -> x8, Pallas kernels: 13.3 us -> 11.8 us  [run(): pl.pallas_call(body, out_shape=outs, in_specs=[pl.BlockSpec(memory_space=...]
  transfers between devices with their start and end apart: 1 -> 0, of which waited for: 1 -> 0; matrix products, arithmetic and copies ran while one was open for 0% -> 0% of each run, Pallas kernels for 0% -> 0%
where the time goes in v3:
time: 144 us
  blocking collectives  131 us (91%)
  Pallas kernels  11.8 us (8%)
    all_to_all x1, blocking collectives, local(): lax.all_to_all(message.reshape(256, 8, LANES), both, 0, 0, tiled=True)  32.8 us
    all_to_all x2, blocking collectives, local(): message = lax.all_to_all(message, 'space', 0, 0, tiled=True)  28.4 us
    all_to_all x1, blocking collectives, local(): lax.all_to_all(message.reshape(768, 2, LANES), both, 0, 0, tiled=True)  25.1 us
    all_to_all x1, blocking collectives, local(): sums = lax.all_to_all(sums, both, 0, 0, tiled=True)  18.7 us
    all_to_all x1, blocking collectives, local(): message = lax.all_to_all(message, 'tm', 0, 0, tiled=True)  13.9 us
    all_to_all x1, blocking collectives, local(): lax.all_to_all(message.reshape(8, TWP, WIDE), 'tm', 0, 0, tiled=True)  12.6 us
    pallas_call x8, Pallas kernels, run(): pl.pallas_call(body, out_shape=outs, in_specs=[pl.BlockSpec(memory_space=...  11.8 us

profile of v3, /device:TPU:1, one launch (start us, length us, event | category | flops | bytes accessed | tf_op | source)
XLA Modules:
  0.0 144.0 jit_solution(10326760515996356573)
XLA Ops:
  0.6 2.0 %prepare.1 = (bf16[8,32,768]{2,1,0:T(8,128)(2,1)S(1)}, bf16[256,256]{1,0:T(8,128)(2,1)S(1)}, bf16[256,256]{1,0:T(8,128)(2,1)S(1)}, f32[16,128]{1,0:T(8,128)S(1)}) custom-call(s32[1,8]{1,0:T(1,128)} %tile_hbm.1, f32[240,720]{1,0:T(8,128)} %bitcast.21, f32[240,240]{1,0:T(8,128)} %factor_hbm.1, f32[720]{0:T(1024)} %conduct_hbm.1), custom_call_target="tpu_custom_call" | custom-call | tf_op jit(solution)/shard_map/prepare/pallas_call | solution.py:35
  2.7 13.9 %all_to_all.41 = bf16[8,32,768]{2,1,0:T(8,128)(2,1)S(1)} all-to-all(bf16[8,32,768]{2,1,0:T(8,128)(2,1)S(1)} %get-tuple-element.15), channel_id=1, replica_groups=mesh['space'=32,'tm'=8] {'tm'}, dimensions={0} | all-to-all | bytes 786432 | tf_op jit(solution)/shard_map/prepare/all_to_all | solution.py:443
  16.5 0.0 copy-start.2
  16.5 0.0 copy-start.4
  16.5 0.9 mix.1
  17.4 32.8 %all_to_all.42 = bf16[256,8,128]{2,1,0:T(8,128)(2,1)S(1)} all-to-all(bf16[256,8,128]{2,1,0:T(8,128)(2,1)S(1)} %bitcast.26), channel_id=1, replica_groups=mesh['space'=32,'tm'=8] {'space','tm'}, dimensions={0} | all-to-all | bytes 1048576 | tf_op jit(solution)/shard_map/mix/all_to_all | solution.py:448
  50.2 1.9 %spread.1 = (bf16[32,8,384]{2,1,0:T(8,128)(2,1)S(1)}, f32[32,768]{1,0:T(8,128)S(1)}, s32[32,128]{1,0:T(8,128)S(1)}) custom-call(bf16[2048,128]{1,0:T(8,128)(2,1)S(1)} %bitcast.27), custom_call_target="tpu_custom_call" | custom-call | tf_op jit(solution)/shard_map/spread/pallas_call | solution.py:35
  52.0 14.1 %all_to_all.43.x_ref = bf16[32,8,384]{2,1,0:T(8,128)(2,1)S(1)} all-to-all(bf16[32,8,384]{2,1,0:T(8,128)(2,1)S(1)} %get-tuple-element.20), channel_id=1, replica_groups=mesh['space'=32,'tm'=8] {'space'}, dimensions={0} | all-to-all | bytes 393216 | tf_op jit(solution)/shard_map/spread/all_to_all | solution.py:461
  66.1 0.0 copy-done.2
  66.1 0.0 copy-done.4
  66.1 1.4 observe.1
  67.5 14.3 %all_to_all.44.x_ref = bf16[32,8,384]{2,1,0:T(8,128)(2,1)S(1)} all-to-all(bf16[32,8,384]{2,1,0:T(8,128)(2,1)S(1)} %observe.1), channel_id=1, replica_groups=mesh['space'=32,'tm'=8] {'space'}, dimensions={0} | all-to-all | bytes 393216 | tf_op jit(solution)/shard_map/observe/all_to_all | solution.py:468
  81.9 0.0 copy-start
  81.9 0.0 copy-start.1
  81.9 2.8 %collect.1 = bf16[1536,128]{1,0:T(8,128)(2,1)S(1)} custom-call(s32[32,128]{1,0:T(8,128)S(1)} %get-tuple-element.19.slot_any, bf16[32,8,384]{2,1,0:T(8,128)(2,1)S(1)} %all_to_all.44.x_ref, f32[32,768]{1,0:T(8,128)S(1)} %get-tuple-element.21.k_ref), custom_call_target="tpu_custom_call" | custom-call | tf_op jit(solution)/shard_map/collect/pallas_call | solution.py:35
  84.7 25.1 %all_to_all.45 = bf16[768,2,128]{2,1,0:T(2,128)(2,1)S(1)} all-to-all(bf16[768,2,128]{2,1,0:T(2,128)(2,1)S(1)} %bitcast.31), channel_id=1, replica_groups=mesh['space'=32,'tm'=8] {'space','tm'}, dimensions={0} | all-to-all | bytes 786432 | tf_op jit(solution)/shard_map/collect/all_to_all | solution.py:482
  109.7 0.7 unmix.1
  110.4 0.0 copy-start.3
  110.4 12.6 %all_to_all.46 = bf16[8,32,768]{2,1,0:T(8,128)(2,1)S(1)} all-to-all(bf16[8,32,768]{2,1,0:T(8,128)(2,1)S(1)} %bitcast.33), channel_id=1, replica_groups=mesh['space'=32,'tm'=8] {'tm'}, dimensions={0} | all-to-all | bytes 786432 | tf_op jit(solution)/shard_map/unmix/all_to_all | solution.py:489
  123.0 0.0 copy-done
  123.0 0.0 copy-done.1
  123.0 0.7 image.1
  123.7 18.7 %all_to_all.47 = f32[256,1,128]{2,1,0:T(1,128)S(1)} all-to-all(f32[256,1,128]{2,1,0:T(1,128)S(1)} %bitcast.36), channel_id=1, replica_groups=mesh['space'=32,'tm'=8] {'space','tm'}, dimensions={0} | all-to-all | bytes 262144 | tf_op jit(solution)/shard_map/image/all_to_all | solution.py:496
  142.4 0.0 copy-done.3
  142.4 1.6 %update.1 = (f32[30,8,720]{2,1,0:T(8,128)}, f32[30,8,720]{2,1,0:T(8,128)}, f32[30,8,720]{2,1,0:T(8,128)}) custom-call(f32[256,128]{1,0:T(8,128)S(1)} %bitcast.35, f32[30,8,720]{2,1,0:T(8,128)S(1)} %bitcast.34, f32[30,8,720]{2,1,0:T(8,128)S(1)} %bitcast.25, f32[30,8,720]{2,1,0:T(8,128)S(1)} %bitcast.23, f32[30,8,720]{2,1,0:T(8,128)S(1)} %get-tuple-element.23.image_ref), custom_call_target="tpu_custom_call" | custom-call | tf_op jit(solution)/shard_map/update/pallas_call | solution.py:35
Async XLA Ops:
  16.5 49.6 %copy-start.2 = (bf16[1,8,64,1440]{3,2,1,0:T(8,128)(2,1)S(1)}, bf16[1,8,64,1440]{3,2,1,0:T(8,128)(2,1)}, u32[]{:S(2)}) copy-start(bf16[1,8,64,1440]{3,2,1,0:T(8,128)(2,1)} %param.14) | copy-start | bytes 4423684
  16.5 49.6 %copy-start.4 = (f32[1,1,64]{2,1,0:T(1,128)S(1)}, f32[1,1,64]{2,1,0:T(1,128)}, u32[]{:S(2)}) copy-start(f32[1,1,64]{2,1,0:T(1,128)} %param.15) | copy-start | bytes 772
  81.9 41.2 %copy-start = (f32[8,30,720]{2,0,1:T(8,128)S(1)}, f32[8,30,720]{2,0,1:T(8,128)}, u32[]{:S(2)}) copy-start(f32[8,30,720]{2,0,1:T(8,128)} %param.10) | copy-start | bytes 2073604
  81.9 41.2 %copy-start.1 = (f32[8,30,720]{2,0,1:T(8,128)S(1)}, f32[8,30,720]{2,0,1:T(8,128)}, u32[]{:S(2)}) copy-start(f32[8,30,720]{2,0,1:T(8,128)} %param.9) | copy-start | bytes 2073604
  110.4 32.0 %copy-start.3 = (f32[8,30,720]{2,0,1:T(8,128)S(1)}, f32[8,30,720]{2,0,1:T(8,128)}, u32[]{:S(2)}) copy-start(f32[8,30,720]{2,0,1:T(8,128)} %param.8) | copy-start | bytes 2073604

commit v4 on v3

--- a/solution.py
+++ b/solution.py
@@ -166,9 +166,8 @@
 
 def mix_body(x_ref, hi_ref, lo_ref, cut_ref, out_ref, z_ref):
     x = x_ref[...]
-    mixed = jnp.dot(hi_ref[...], x, preferred_element_type=F32) + jnp.dot(
-        lo_ref[...], x, preferred_element_type=F32
-    )
+    parts = jnp.dot(jnp.concatenate([hi_ref[...], lo_ref[...]], axis=0), x, preferred_element_type=F32)
+    mixed = parts[0:256] + parts[256:512]
     m = lax.axis_index("tm")
     for e in range(2):
         part = cut_ref[pl.ds(2 * m + e, 1), :]
@@ -199,13 +198,21 @@
     return value[:, q * LANES : (q + 1) * LANES]
 
 
+def moved(take, source, target, lane):
+    a, first = source // LANES, source % LANES
+    cells = take(a)
+    if first + TC > LANES:
+        cells = jnp.where(lane >= first, cells, take(a + 1))
+    return turn(cells, target - source)
+
+
 def spread_body(x_ref, out_ref, kept_ref, code_ref, z_ref, w_ref, table_ref, slot_ref, sem):
     lane = lanes_of((8, LANES))
     z_ref[0:2048, :] = x_ref[...].astype(F32)
     codes = z_ref[pl.ds(PIECES - 1, ROWS, stride=64), :]
     line = lanes_of((ROWS, LANES))
-    codes = jnp.where((line >= IDX) & (line < IDX + NB), turn(codes, -NB) * ROWS + codes, 0.0)
-    code_ref[...] = codes.astype(jnp.int32)
+    codes = jnp.where(line < NB, turn(codes, -IDX - NB) * ROWS + turn(codes, -IDX), 0.0)
+    code_ref[...] = jnp.transpose(codes)[0:NB, :].astype(jnp.int32)
     slot_copy = pltpu.make_async_copy(code_ref, slot_ref, sem)
     slot_copy.start()
     for q in range(PIECES):
@@ -223,10 +230,7 @@
 
     def cut(s, value):
         for c in range(COLS):
-            parts = [
-                (low, high, turn(piece(value, a), rotation)) for a, _, low, high, rotation in span(0, c * TC)
-            ]
-            table_ref[c * ROWS + s] = chain(parts, lane)
+            table_ref[c * ROWS + s] = moved(lambda a: piece(value, a), c * TC, 0, lane)
 
     sweep(arrived, kept_ref, keep)
     sweep(lambda s: w_ref[s], kept_ref, keep)
@@ -239,7 +243,7 @@
     waiting = {}
     for s in range(ROWS + ahead):
         if s < ROWS:
-            waiting[s] = [table_ref[slot_ref[s, IDX + j]] for j in range(NB)]
+            waiting[s] = [table_ref[slot_ref[j, s]] for j in range(NB)]
         if s >= ahead:
             tiles = waiting.pop(s - ahead)
             runs = [[], [], []]
@@ -256,9 +260,9 @@
     for tau in range(TW):
         value = x_ref[tau].astype(F32)
         for j in range(NB):
-            for a, b, low, high, rotation in span(tau * TC, j * TC):
-                piece = turn(value[:, a * LANES : (a + 1) * LANES], rotation)
-                runs.setdefault((j, b), []).append((low, high, piece))
+            cells = moved(lambda a: piece(value, a), j * TC, tau * TC, lane)
+            for _, b, low, high, _ in span(tau * TC, 0):
+                runs.setdefault((j, b), []).append((low, high, cells))
         for key in [key for key in runs if (key[1] + 1) * LANES <= (tau + 1) * TC or tau == TW - 1]:
             j, b = key
             x2_ref[j, :, b * LANES : (b + 1) * LANES] = chain(runs.pop(key), lane)
@@ -276,8 +280,9 @@
     for tau in range(TW):
         runs = [[], [], []]
         for j in range(NB):
-            for a, b, low, high, rotation in span(j * TC, tau * TC):
-                runs[b].append((low, high, turn(g_ref[j, :, a * LANES : (a + 1) * LANES], rotation)))
+            cells = moved(lambda a: g_ref[j, :, a * LANES : (a + 1) * LANES], tau * TC, j * TC, lane)
+            for _, b, low, high, _ in span(j * TC, 0):
+                runs[b].append((low, high, cells))
         for b in range(3):
             out_ref[tau, :, b * LANES : (b + 1) * LANES] = chain(runs[b], lane).astype(BF16)
     out_ref[TW:TWP] = jnp.zeros((TWP - TW, 8, NB * TC), BF16)
@@ -292,11 +297,10 @@
 
     def reader(s, carry):
         value = x_ref[s].astype(F32)
-        tiles = [slot_ref[s, IDX + j] for j in range(NB)]
+        tiles = [slot_ref[j, s] for j in range(NB)]
         sums = []
         for j in range(NB):
-            parts = [(low, high, turn(piece(value, a), rotation)) for a, _, low, high, rotation in span(0, j * TC)]
-            sums.append(table_ref[tiles[j]] + chain(parts, lane))
+            sums.append(table_ref[tiles[j]] + moved(lambda a: piece(value, a), j * TC, 0, lane))
         for j in range(NB):
             table_ref[tiles[j]] = sums[j]
         return carry
@@ -449,12 +453,12 @@
     with jax.named_scope("spread"):
         message, conduct, slots = call(
             spread_body,
-            (shape((ROWS, 8, NB * TC), BF16), shape((ROWS, WIDE), F32), shape((ROWS, LANES), jnp.int32)),
+            (shape((ROWS, 8, NB * TC), BF16), shape((ROWS, WIDE), F32), shape((NB, ROWS), jnp.int32)),
             [
                 pltpu.VMEM((2112, LANES), F32),
                 pltpu.VMEM(grid, F32),
                 pltpu.VMEM((BLANK + 1, 8, LANES), F32),
-                pltpu.SMEM((ROWS, LANES), jnp.int32),
+                pltpu.SMEM((NB, ROWS), jnp.int32),
                 pltpu.SemaphoreType.DMA,
             ],
         )(message.reshape(2048, LANES))
@@ -474,7 +478,7 @@
                 pltpu.VMEM((1584, LANES), F32),
                 pltpu.VMEM(grid, F32),
                 pltpu.VMEM((BLANK + 1, 8, LANES), F32),
-                pltpu.SMEM((ROWS, LANES), jnp.int32),
+                pltpu.SMEM((NB, ROWS), jnp.int32),
                 pltpu.SemaphoreType.DMA,
             ],
             "h",

time: 144 us -> 144 us (level)
  no operation moved by 1% of the time
where the time goes in v4:
time: 144 us
  blocking collectives  131 us (91%)
  Pallas kernels  11.4 us (8%)
    all_to_all x1, blocking collectives, local(): lax.all_to_all(message.reshape(256, 8, LANES), both, 0, 0, tiled=True)  32.8 us
    all_to_all x2, blocking collectives, local(): message = lax.all_to_all(message, 'space', 0, 0, tiled=True)  28.4 us
    all_to_all x1, blocking collectives, local(): lax.all_to_all(message.reshape(768, 2, LANES), both, 0, 0, tiled=True)  25.1 us
    all_to_all x1, blocking collectives, local(): sums = lax.all_to_all(sums, both, 0, 0, tiled=True)  18.7 us
    all_to_all x1, blocking collectives, local(): message = lax.all_to_all(message, 'tm', 0, 0, tiled=True)  13.9 us
    all_to_all x1, blocking collectives, local(): lax.all_to_all(message.reshape(8, TWP, WIDE), 'tm', 0, 0, tiled=True)  12.6 us
    pallas_call x8, Pallas kernels, run(): pl.pallas_call(body, out_shape=outs, in_specs=[pl.BlockSpec(memory_space=...  11.4 us

profile of v4, /device:TPU:1, one launch (start us, length us, event | category | flops | bytes accessed | tf_op | source)
XLA Modules:
  0.0 143.6 jit_solution(7655217927560742400)
XLA Ops:
  0.6 2.0 %prepare.1 = (bf16[8,32,768]{2,1,0:T(8,128)(2,1)S(1)}, bf16[256,256]{1,0:T(8,128)(2,1)S(1)}, bf16[256,256]{1,0:T(8,128)(2,1)S(1)}, f32[16,128]{1,0:T(8,128)S(1)}) custom-call(s32[1,8]{1,0:T(1,128)} %tile_hbm.1, f32[240,720]{1,0:T(8,128)} %bitcast.21, f32[240,240]{1,0:T(8,128)} %factor_hbm.1, f32[720]{0:T(1024)} %conduct_hbm.1), custom_call_target="tpu_custom_call" | custom-call | tf_op jit(solution)/shard_map/prepare/pallas_call | solution.py:35
  2.7 13.9 %all_to_all.41 = bf16[8,32,768]{2,1,0:T(8,128)(2,1)S(1)} all-to-all(bf16[8,32,768]{2,1,0:T(8,128)(2,1)S(1)} %get-tuple-element.15), channel_id=1, replica_groups=mesh['space'=32,'tm'=8] {'tm'}, dimensions={0} | all-to-all | bytes 786432 | tf_op jit(solution)/shard_map/prepare/all_to_all | solution.py:447
  16.5 0.0 copy-start.2
  16.5 0.0 copy-start.4
  16.5 0.8 mix.1
  17.3 32.8 %all_to_all.42 = bf16[256,8,128]{2,1,0:T(8,128)(2,1)S(1)} all-to-all(bf16[256,8,128]{2,1,0:T(8,128)(2,1)S(1)} %bitcast.26), channel_id=1, replica_groups=mesh['space'=32,'tm'=8] {'space','tm'}, dimensions={0} | all-to-all | bytes 1048576 | tf_op jit(solution)/shard_map/mix/all_to_all | solution.py:452
  50.1 1.7 %spread.1 = (bf16[32,8,384]{2,1,0:T(8,128)(2,1)S(1)}, f32[32,768]{1,0:T(8,128)S(1)}, s32[8,32]{1,0:T(8,128)S(1)}) custom-call(bf16[2048,128]{1,0:T(8,128)(2,1)S(1)} %bitcast.27), custom_call_target="tpu_custom_call" | custom-call | tf_op jit(solution)/shard_map/spread/pallas_call | solution.py:35
  51.8 14.1 %all_to_all.43.x_ref = bf16[32,8,384]{2,1,0:T(8,128)(2,1)S(1)} all-to-all(bf16[32,8,384]{2,1,0:T(8,128)(2,1)S(1)} %get-tuple-element.20), channel_id=1, replica_groups=mesh['space'=32,'tm'=8] {'space'}, dimensions={0} | all-to-all | bytes 393216 | tf_op jit(solution)/shard_map/spread/all_to_all | solution.py:465
  65.9 0.0 copy-done.2
  65.9 0.0 copy-done.4
  66.0 1.4 observe.1
  67.3 14.3 %all_to_all.44.x_ref = bf16[32,8,384]{2,1,0:T(8,128)(2,1)S(1)} all-to-all(bf16[32,8,384]{2,1,0:T(8,128)(2,1)S(1)} %observe.1), channel_id=1, replica_groups=mesh['space'=32,'tm'=8] {'space'}, dimensions={0} | all-to-all | bytes 393216 | tf_op jit(solution)/shard_map/observe/all_to_all | solution.py:472
  81.7 0.0 copy-start
  81.7 0.0 copy-start.1
  81.7 2.6 %collect.1 = bf16[1536,128]{1,0:T(8,128)(2,1)S(1)} custom-call(s32[8,32]{1,0:T(8,128)S(1)} %get-tuple-element.19.slot_any, bf16[32,8,384]{2,1,0:T(8,128)(2,1)S(1)} %all_to_all.44.x_ref, f32[32,768]{1,0:T(8,128)S(1)} %get-tuple-element.21.k_ref), custom_call_target="tpu_custom_call" | custom-call | tf_op jit(solution)/shard_map/collect/pallas_call | solution.py:35
  84.3 25.1 %all_to_all.45 = bf16[768,2,128]{2,1,0:T(2,128)(2,1)S(1)} all-to-all(bf16[768,2,128]{2,1,0:T(2,128)(2,1)S(1)} %bitcast.31), channel_id=1, replica_groups=mesh['space'=32,'tm'=8] {'space','tm'}, dimensions={0} | all-to-all | bytes 786432 | tf_op jit(solution)/shard_map/collect/all_to_all | solution.py:486
  109.3 0.7 unmix.1
  110.0 0.0 copy-start.3
  110.0 12.6 %all_to_all.46 = bf16[8,32,768]{2,1,0:T(8,128)(2,1)S(1)} all-to-all(bf16[8,32,768]{2,1,0:T(8,128)(2,1)S(1)} %bitcast.33), channel_id=1, replica_groups=mesh['space'=32,'tm'=8] {'tm'}, dimensions={0} | all-to-all | bytes 786432 | tf_op jit(solution)/shard_map/unmix/all_to_all | solution.py:493
  122.7 0.0 copy-done
  122.7 0.0 copy-done.1
  122.7 0.7 image.1
  123.3 18.7 %all_to_all.47 = f32[256,1,128]{2,1,0:T(1,128)S(1)} all-to-all(f32[256,1,128]{2,1,0:T(1,128)S(1)} %bitcast.36), channel_id=1, replica_groups=mesh['space'=32,'tm'=8] {'space','tm'}, dimensions={0} | all-to-all | bytes 262144 | tf_op jit(solution)/shard_map/image/all_to_all | solution.py:500
  142.0 0.0 copy-done.3
  142.0 1.6 %update.1 = (f32[30,8,720]{2,1,0:T(8,128)}, f32[30,8,720]{2,1,0:T(8,128)}, f32[30,8,720]{2,1,0:T(8,128)}) custom-call(f32[256,128]{1,0:T(8,128)S(1)} %bitcast.35, f32[30,8,720]{2,1,0:T(8,128)S(1)} %bitcast.34, f32[30,8,720]{2,1,0:T(8,128)S(1)} %bitcast.25, f32[30,8,720]{2,1,0:T(8,128)S(1)} %bitcast.23, f32[30,8,720]{2,1,0:T(8,128)S(1)} %get-tuple-element.23.image_ref), custom_call_target="tpu_custom_call" | custom-call | tf_op jit(solution)/shard_map/update/pallas_call | solution.py:35
Async XLA Ops:
  16.5 49.4 %copy-start.2 = (bf16[1,8,64,1440]{3,2,1,0:T(8,128)(2,1)S(1)}, bf16[1,8,64,1440]{3,2,1,0:T(8,128)(2,1)}, u32[]{:S(2)}) copy-start(bf16[1,8,64,1440]{3,2,1,0:T(8,128)(2,1)} %param.14) | copy-start | bytes 4423684
  16.5 49.4 %copy-start.4 = (f32[1,1,64]{2,1,0:T(1,128)S(1)}, f32[1,1,64]{2,1,0:T(1,128)}, u32[]{:S(2)}) copy-start(f32[1,1,64]{2,1,0:T(1,128)} %param.15) | copy-start | bytes 772
  81.7 41.0 %copy-start = (f32[8,30,720]{2,0,1:T(8,128)S(1)}, f32[8,30,720]{2,0,1:T(8,128)}, u32[]{:S(2)}) copy-start(f32[8,30,720]{2,0,1:T(8,128)} %param.10) | copy-start | bytes 2073604
  81.7 41.0 %copy-start.1 = (f32[8,30,720]{2,0,1:T(8,128)S(1)}, f32[8,30,720]{2,0,1:T(8,128)}, u32[]{:S(2)}) copy-start(f32[8,30,720]{2,0,1:T(8,128)} %param.9) | copy-start | bytes 2073604
  110.0 32.0 %copy-start.3 = (f32[8,30,720]{2,0,1:T(8,128)S(1)}, f32[8,30,720]{2,0,1:T(8,128)}, u32[]{:S(2)}) copy-start(f32[8,30,720]{2,0,1:T(8,128)} %param.8) | copy-start | bytes 2073604

commit v5 on v4

--- a/solution.py
+++ b/solution.py
@@ -288,19 +288,22 @@
     out_ref[TW:TWP] = jnp.zeros((TWP - TW, 8, NB * TC), BF16)
 
 
-def collect_body(slot_any, x_ref, k_ref, out_ref, z_ref, w_ref, table_ref, slot_ref, sem):
+def collect_body(slot_any, x_ref, k_ref, out_ref, z_ref, w_ref, table_ref, pieces_ref, slot_ref, sem):
     slot_copy = pltpu.make_async_copy(slot_any, slot_ref, sem)
     slot_copy.start()
     lane = lanes_of((8, LANES))
     table_ref[...] = jnp.zeros(table_ref.shape, F32)
+    for s in range(ROWS):
+        value = x_ref[s].astype(F32)
+        for j in range(NB):
+            pieces_ref[s * NB + j] = moved(lambda a: piece(value, a), j * TC, 0, lane)
     slot_copy.wait()
 
     def reader(s, carry):
-        value = x_ref[s].astype(F32)
         tiles = [slot_ref[j, s] for j in range(NB)]
         sums = []
         for j in range(NB):
-            sums.append(table_ref[tiles[j]] + moved(lambda a: piece(value, a), j * TC, 0, lane))
+            sums.append(table_ref[tiles[j]] + pieces_ref[s * NB + j])
         for j in range(NB):
             table_ref[tiles[j]] = sums[j]
         return carry
@@ -385,17 +388,15 @@
     step = rr / dq
     norm = jnp.maximum(rr + step * (step * qq - 2.0 * rq), 0.0)
     ratio = norm / rr
-    count = 3
-    rows = TW // count
     copies = []
-    for i in range(count):
-        for t in range(i * rows, (i + 1) * rows):
+    for i, (start, stop) in enumerate(((0, 3), (3, 12), (12, 21), (21, TW))):
+        for t in range(start, stop):
             d = d_ref[t]
             after = r_ref[t] - step * image_ref[t]
             it_new[t] = it_ref[t] + step * d
             r_new[t] = after
             d_new[t] = after + ratio * d
-        at = pl.ds(i * rows, rows)
+        at = pl.ds(start, stop - start)
         for n, (new, out) in enumerate(((it_new, it_out), (r_new, r_out), (d_new, d_out))):
             copies.append(pltpu.make_async_copy(new.at[at], out.at[at], sem.at[n, i]))
             copies[-1].start()
@@ -478,6 +479,7 @@
                 pltpu.VMEM((1584, LANES), F32),
                 pltpu.VMEM(grid, F32),
                 pltpu.VMEM((BLANK + 1, 8, LANES), F32),
+                pltpu.VMEM((ROWS * NB, 8, LANES), F32),
                 pltpu.SMEM((NB, ROWS), jnp.int32),
                 pltpu.SemaphoreType.DMA,
             ],
@@ -503,7 +505,7 @@
         outs = call(
             update_body,
             tuple(shape(whole, F32) for _ in range(3)),
-            [pltpu.VMEM(whole, F32) for _ in range(3)] + [pltpu.SemaphoreType.DMA((3, 3))],
+            [pltpu.VMEM(whole, F32) for _ in range(3)] + [pltpu.SemaphoreType.DMA((3, 4))],
             out_places="hhh",
         )(sums, iterate, residual, direction, image)
     return tuple(jnp.transpose(value, (1, 0, 2)) for value in outs)

time: 144 us -> 144 us (level)
  no operation moved by 1% of the time
where the time goes in v5:
time: 144 us
  blocking collectives  131 us (91%)
  Pallas kernels  11.4 us (8%)
    all_to_all x1, blocking collectives, local(): lax.all_to_all(message.reshape(256, 8, LANES), both, 0, 0, tiled=True)  32.8 us
    all_to_all x2, blocking collectives, local(): message = lax.all_to_all(message, 'space', 0, 0, tiled=True)  28.4 us
    all_to_all x1, blocking collectives, local(): lax.all_to_all(message.reshape(768, 2, LANES), both, 0, 0, tiled=True)  25.1 us
    all_to_all x1, blocking collectives, local(): sums = lax.all_to_all(sums, both, 0, 0, tiled=True)  18.7 us
    all_to_all x1, blocking collectives, local(): message = lax.all_to_all(message, 'tm', 0, 0, tiled=True)  13.9 us
    all_to_all x1, blocking collectives, local(): lax.all_to_all(message.reshape(8, TWP, WIDE), 'tm', 0, 0, tiled=True)  12.6 us
    pallas_call x8, Pallas kernels, run(): pl.pallas_call(body, out_shape=outs, in_specs=[pl.BlockSpec(memory_space=...  11.4 us

profile of v5, /device:TPU:1, one launch (start us, length us, event | category | flops | bytes accessed | tf_op | source)
XLA Modules:
  0.0 143.6 jit_solution(4217793602142605677)
XLA Ops:
  0.6 2.0 %prepare.1 = (bf16[8,32,768]{2,1,0:T(8,128)(2,1)S(1)}, bf16[256,256]{1,0:T(8,128)(2,1)S(1)}, bf16[256,256]{1,0:T(8,128)(2,1)S(1)}, f32[16,128]{1,0:T(8,128)S(1)}) custom-call(s32[1,8]{1,0:T(1,128)} %tile_hbm.1, f32[240,720]{1,0:T(8,128)} %bitcast.21, f32[240,240]{1,0:T(8,128)} %factor_hbm.1, f32[720]{0:T(1024)} %conduct_hbm.1), custom_call_target="tpu_custom_call" | custom-call | tf_op jit(solution)/shard_map/prepare/pallas_call | solution.py:35
  2.7 13.9 %all_to_all.41 = bf16[8,32,768]{2,1,0:T(8,128)(2,1)S(1)} all-to-all(bf16[8,32,768]{2,1,0:T(8,128)(2,1)S(1)} %get-tuple-element.15), channel_id=1, replica_groups=mesh['space'=32,'tm'=8] {'tm'}, dimensions={0} | all-to-all | bytes 786432 | tf_op jit(solution)/shard_map/prepare/all_to_all | solution.py:448
  16.5 0.0 copy-start.2
  16.5 0.0 copy-start.4
  16.5 0.8 mix.1
  17.3 32.8 %all_to_all.42 = bf16[256,8,128]{2,1,0:T(8,128)(2,1)S(1)} all-to-all(bf16[256,8,128]{2,1,0:T(8,128)(2,1)S(1)} %bitcast.26), channel_id=1, replica_groups=mesh['space'=32,'tm'=8] {'space','tm'}, dimensions={0} | all-to-all | bytes 1048576 | tf_op jit(solution)/shard_map/mix/all_to_all | solution.py:453
  50.1 1.7 %spread.1 = (bf16[32,8,384]{2,1,0:T(8,128)(2,1)S(1)}, f32[32,768]{1,0:T(8,128)S(1)}, s32[8,32]{1,0:T(8,128)S(1)}) custom-call(bf16[2048,128]{1,0:T(8,128)(2,1)S(1)} %bitcast.27), custom_call_target="tpu_custom_call" | custom-call | tf_op jit(solution)/shard_map/spread/pallas_call | solution.py:35
  51.8 14.1 %all_to_all.43.x_ref = bf16[32,8,384]{2,1,0:T(8,128)(2,1)S(1)} all-to-all(bf16[32,8,384]{2,1,0:T(8,128)(2,1)S(1)} %get-tuple-element.20), channel_id=1, replica_groups=mesh['space'=32,'tm'=8] {'space'}, dimensions={0} | all-to-all | bytes 393216 | tf_op jit(solution)/shard_map/spread/all_to_all | solution.py:466
  65.9 0.0 copy-done.2
  65.9 0.0 copy-done.4
  66.0 1.4 observe.1
  67.3 14.3 %all_to_all.44.x_ref = bf16[32,8,384]{2,1,0:T(8,128)(2,1)S(1)} all-to-all(bf16[32,8,384]{2,1,0:T(8,128)(2,1)S(1)} %observe.1), channel_id=1, replica_groups=mesh['space'=32,'tm'=8] {'space'}, dimensions={0} | all-to-all | bytes 393216 | tf_op jit(solution)/shard_map/observe/all_to_all | solution.py:473
  81.7 0.0 copy-start
  81.7 0.0 copy-start.1
  81.7 2.5 %collect.1 = bf16[1536,128]{1,0:T(8,128)(2,1)S(1)} custom-call(s32[8,32]{1,0:T(8,128)S(1)} %get-tuple-element.19.slot_any, bf16[32,8,384]{2,1,0:T(8,128)(2,1)S(1)} %all_to_all.44.x_ref, f32[32,768]{1,0:T(8,128)S(1)} %get-tuple-element.21.k_ref), custom_call_target="tpu_custom_call" | custom-call | tf_op jit(solution)/shard_map/collect/pallas_call | solution.py:35
  84.2 25.1 %all_to_all.45 = bf16[768,2,128]{2,1,0:T(2,128)(2,1)S(1)} all-to-all(bf16[768,2,128]{2,1,0:T(2,128)(2,1)S(1)} %bitcast.31), channel_id=1, replica_groups=mesh['space'=32,'tm'=8] {'space','tm'}, dimensions={0} | all-to-all | bytes 786432 | tf_op jit(solution)/shard_map/collect/all_to_all | solution.py:488
  109.3 0.7 unmix.1
  109.9 0.0 copy-start.3
  110.0 12.6 %all_to_all.46 = bf16[8,32,768]{2,1,0:T(8,128)(2,1)S(1)} all-to-all(bf16[8,32,768]{2,1,0:T(8,128)(2,1)S(1)} %bitcast.33), channel_id=1, replica_groups=mesh['space'=32,'tm'=8] {'tm'}, dimensions={0} | all-to-all | bytes 786432 | tf_op jit(solution)/shard_map/unmix/all_to_all | solution.py:495
  122.6 0.0 copy-done
  122.6 0.0 copy-done.1
  122.6 0.7 image.1
  123.3 18.7 %all_to_all.47 = f32[256,1,128]{2,1,0:T(1,128)S(1)} all-to-all(f32[256,1,128]{2,1,0:T(1,128)S(1)} %bitcast.36), channel_id=1, replica_groups=mesh['space'=32,'tm'=8] {'space','tm'}, dimensions={0} | all-to-all | bytes 262144 | tf_op jit(solution)/shard_map/image/all_to_all | solution.py:502
  142.0 0.0 copy-done.3
  142.0 1.6 %update.1 = (f32[30,8,720]{2,1,0:T(8,128)}, f32[30,8,720]{2,1,0:T(8,128)}, f32[30,8,720]{2,1,0:T(8,128)}) custom-call(f32[256,128]{1,0:T(8,128)S(1)} %bitcast.35, f32[30,8,720]{2,1,0:T(8,128)S(1)} %bitcast.34, f32[30,8,720]{2,1,0:T(8,128)S(1)} %bitcast.25, f32[30,8,720]{2,1,0:T(8,128)S(1)} %bitcast.23, f32[30,8,720]{2,1,0:T(8,128)S(1)} %get-tuple-element.23.image_ref), custom_call_target="tpu_custom_call" | custom-call | tf_op jit(solution)/shard_map/update/pallas_call | solution.py:35
Async XLA Ops:
  16.5 49.4 %copy-start.2 = (bf16[1,8,64,1440]{3,2,1,0:T(8,128)(2,1)S(1)}, bf16[1,8,64,1440]{3,2,1,0:T(8,128)(2,1)}, u32[]{:S(2)}) copy-start(bf16[1,8,64,1440]{3,2,1,0:T(8,128)(2,1)} %param.14) | copy-start | bytes 4423684
  16.5 49.4 %copy-start.4 = (f32[1,1,64]{2,1,0:T(1,128)S(1)}, f32[1,1,64]{2,1,0:T(1,128)}, u32[]{:S(2)}) copy-start(f32[1,1,64]{2,1,0:T(1,128)} %param.15) | copy-start | bytes 772
  81.7 40.9 %copy-start = (f32[8,30,720]{2,0,1:T(8,128)S(1)}, f32[8,30,720]{2,0,1:T(8,128)}, u32[]{:S(2)}) copy-start(f32[8,30,720]{2,0,1:T(8,128)} %param.10) | copy-start | bytes 2073604
  81.7 40.9 %copy-start.1 = (f32[8,30,720]{2,0,1:T(8,128)S(1)}, f32[8,30,720]{2,0,1:T(8,128)}, u32[]{:S(2)}) copy-start(f32[8,30,720]{2,0,1:T(8,128)} %param.9) | copy-start | bytes 2073604
  109.9 32.0 %copy-start.3 = (f32[8,30,720]{2,0,1:T(8,128)S(1)}, f32[8,30,720]{2,0,1:T(8,128)}, u32[]{:S(2)}) copy-start(f32[8,30,720]{2,0,1:T(8,128)} %param.8) | copy-start | bytes 2073604

commit v6 on v5

--- a/solution.py
+++ b/solution.py
@@ -182,14 +182,14 @@
     before, here, conduct = None, load(0), k_ref[0:1, :]
     u = here * conduct
     for s in range(ROWS):
-        laplace = turn(u, 1) + turn(u, -1) - 4.0 * u
+        around = turn(u, 1) + turn(u, -1)
         if before is not None:
-            laplace = laplace + before
+            around = around + before
         if s + 1 < ROWS:
             after, conduct_after = load(s + 1), k_ref[s + 1 : s + 2, :]
             u_after = after * conduct_after
-            laplace = laplace + u_after
-        store(s, here + conduct * laplace)
+            around = around + u_after
+        store(s, (1.0 - 4.0 * conduct * conduct) * here + conduct * around)
         if s + 1 < ROWS:
             before, here, conduct, u = u, after, conduct_after, u_after
 

time: 144 us -> 144 us (level)
  no operation moved by 1% of the time
where the time goes in v6:
time: 144 us; the launch traced here: 143 us
  blocking collectives  131 us (91%)
  Pallas kernels  11.3 us (8%)
    all_to_all x1, blocking collectives, local(): lax.all_to_all(message.reshape(256, 8, LANES), both, 0, 0, tiled=True)  32.8 us
    all_to_all x2, blocking collectives, local(): message = lax.all_to_all(message, 'space', 0, 0, tiled=True)  28.4 us
    all_to_all x1, blocking collectives, local(): lax.all_to_all(message.reshape(768, 2, LANES), both, 0, 0, tiled=True)  25.1 us
    all_to_all x1, blocking collectives, local(): sums = lax.all_to_all(sums, both, 0, 0, tiled=True)  18.7 us
    all_to_all x1, blocking collectives, local(): message = lax.all_to_all(message, 'tm', 0, 0, tiled=True)  13.9 us
    all_to_all x1, blocking collectives, local(): lax.all_to_all(message.reshape(8, TWP, WIDE), 'tm', 0, 0, tiled=True)  12.6 us
    pallas_call x8, Pallas kernels, run(): pl.pallas_call(body, out_shape=outs, in_specs=[pl.BlockSpec(memory_space=...  11.3 us

profile of v6, /device:TPU:1, one launch (start us, length us, event | category | flops | bytes accessed | tf_op | source)
XLA Modules:
  0.0 143.5 jit_solution(2845502969813344559)
XLA Ops:
  0.6 2.0 %prepare.1 = (bf16[8,32,768]{2,1,0:T(8,128)(2,1)S(1)}, bf16[256,256]{1,0:T(8,128)(2,1)S(1)}, bf16[256,256]{1,0:T(8,128)(2,1)S(1)}, f32[16,128]{1,0:T(8,128)S(1)}) custom-call(s32[1,8]{1,0:T(1,128)} %tile_hbm.1, f32[240,720]{1,0:T(8,128)} %bitcast.21, f32[240,240]{1,0:T(8,128)} %factor_hbm.1, f32[720]{0:T(1024)} %conduct_hbm.1), custom_call_target="tpu_custom_call" | custom-call | tf_op jit(solution)/shard_map/prepare/pallas_call | solution.py:35
  2.7 13.9 %all_to_all.41 = bf16[8,32,768]{2,1,0:T(8,128)(2,1)S(1)} all-to-all(bf16[8,32,768]{2,1,0:T(8,128)(2,1)S(1)} %get-tuple-element.15), channel_id=1, replica_groups=mesh['space'=32,'tm'=8] {'tm'}, dimensions={0} | all-to-all | bytes 786432 | tf_op jit(solution)/shard_map/prepare/all_to_all | solution.py:448
  16.5 0.0 copy-start.2
  16.5 0.0 copy-start.4
  16.5 0.8 mix.1
  17.3 32.8 %all_to_all.42 = bf16[256,8,128]{2,1,0:T(8,128)(2,1)S(1)} all-to-all(bf16[256,8,128]{2,1,0:T(8,128)(2,1)S(1)} %bitcast.26), channel_id=1, replica_groups=mesh['space'=32,'tm'=8] {'space','tm'}, dimensions={0} | all-to-all | bytes 1048576 | tf_op jit(solution)/shard_map/mix/all_to_all | solution.py:453
  50.1 1.7 %spread.1 = (bf16[32,8,384]{2,1,0:T(8,128)(2,1)S(1)}, f32[32,768]{1,0:T(8,128)S(1)}, s32[8,32]{1,0:T(8,128)S(1)}) custom-call(bf16[2048,128]{1,0:T(8,128)(2,1)S(1)} %bitcast.27), custom_call_target="tpu_custom_call" | custom-call | tf_op jit(solution)/shard_map/spread/pallas_call | solution.py:35
  51.8 14.1 %all_to_all.43.x_ref = bf16[32,8,384]{2,1,0:T(8,128)(2,1)S(1)} all-to-all(bf16[32,8,384]{2,1,0:T(8,128)(2,1)S(1)} %get-tuple-element.20), channel_id=1, replica_groups=mesh['space'=32,'tm'=8] {'space'}, dimensions={0} | all-to-all | bytes 393216 | tf_op jit(solution)/shard_map/spread/all_to_all | solution.py:466
  65.9 0.0 copy-done.2
  65.9 0.0 copy-done.4
  65.9 1.4 observe.1
  67.3 14.3 %all_to_all.44.x_ref = bf16[32,8,384]{2,1,0:T(8,128)(2,1)S(1)} all-to-all(bf16[32,8,384]{2,1,0:T(8,128)(2,1)S(1)} %observe.1), channel_id=1, replica_groups=mesh['space'=32,'tm'=8] {'space'}, dimensions={0} | all-to-all | bytes 393216 | tf_op jit(solution)/shard_map/observe/all_to_all | solution.py:473
  81.7 0.0 copy-start
  81.7 0.0 copy-start.1
  81.7 2.4 %collect.1 = bf16[1536,128]{1,0:T(8,128)(2,1)S(1)} custom-call(s32[8,32]{1,0:T(8,128)S(1)} %get-tuple-element.19.slot_any, bf16[32,8,384]{2,1,0:T(8,128)(2,1)S(1)} %all_to_all.44.x_ref, f32[32,768]{1,0:T(8,128)S(1)} %get-tuple-element.21.k_ref), custom_call_target="tpu_custom_call" | custom-call | tf_op jit(solution)/shard_map/collect/pallas_call | solution.py:35
  84.1 25.1 %all_to_all.45 = bf16[768,2,128]{2,1,0:T(2,128)(2,1)S(1)} all-to-all(bf16[768,2,128]{2,1,0:T(2,128)(2,1)S(1)} %bitcast.31), channel_id=1, replica_groups=mesh['space'=32,'tm'=8] {'space','tm'}, dimensions={0} | all-to-all | bytes 786432 | tf_op jit(solution)/shard_map/collect/all_to_all | solution.py:488
  109.2 0.7 unmix.1
  109.8 0.0 copy-start.3
  109.9 12.6 %all_to_all.46 = bf16[8,32,768]{2,1,0:T(8,128)(2,1)S(1)} all-to-all(bf16[8,32,768]{2,1,0:T(8,128)(2,1)S(1)} %bitcast.33), channel_id=1, replica_groups=mesh['space'=32,'tm'=8] {'tm'}, dimensions={0} | all-to-all | bytes 786432 | tf_op jit(solution)/shard_map/unmix/all_to_all | solution.py:495
  122.5 0.0 copy-done
  122.5 0.0 copy-done.1
  122.5 0.7 image.1
  123.2 18.7 %all_to_all.47 = f32[256,1,128]{2,1,0:T(1,128)S(1)} all-to-all(f32[256,1,128]{2,1,0:T(1,128)S(1)} %bitcast.36), channel_id=1, replica_groups=mesh['space'=32,'tm'=8] {'space','tm'}, dimensions={0} | all-to-all | bytes 262144 | tf_op jit(solution)/shard_map/image/all_to_all | solution.py:502
  141.9 0.0 copy-done.3
  141.9 1.6 %update.1 = (f32[30,8,720]{2,1,0:T(8,128)}, f32[30,8,720]{2,1,0:T(8,128)}, f32[30,8,720]{2,1,0:T(8,128)}) custom-call(f32[256,128]{1,0:T(8,128)S(1)} %bitcast.35, f32[30,8,720]{2,1,0:T(8,128)S(1)} %bitcast.34, f32[30,8,720]{2,1,0:T(8,128)S(1)} %bitcast.25, f32[30,8,720]{2,1,0:T(8,128)S(1)} %bitcast.23, f32[30,8,720]{2,1,0:T(8,128)S(1)} %get-tuple-element.23.image_ref), custom_call_target="tpu_custom_call" | custom-call | tf_op jit(solution)/shard_map/update/pallas_call | solution.py:35
Async XLA Ops:
  16.5 49.4 %copy-start.2 = (bf16[1,8,64,1440]{3,2,1,0:T(8,128)(2,1)S(1)}, bf16[1,8,64,1440]{3,2,1,0:T(8,128)(2,1)}, u32[]{:S(2)}) copy-start(bf16[1,8,64,1440]{3,2,1,0:T(8,128)(2,1)} %param.14) | copy-start | bytes 4423684
  16.5 49.4 %copy-start.4 = (f32[1,1,64]{2,1,0:T(1,128)S(1)}, f32[1,1,64]{2,1,0:T(1,128)}, u32[]{:S(2)}) copy-start(f32[1,1,64]{2,1,0:T(1,128)} %param.15) | copy-start | bytes 772
  81.7 40.8 %copy-start = (f32[8,30,720]{2,0,1:T(8,128)S(1)}, f32[8,30,720]{2,0,1:T(8,128)}, u32[]{:S(2)}) copy-start(f32[8,30,720]{2,0,1:T(8,128)} %param.10) | copy-start | bytes 2073604
  81.7 40.8 %copy-start.1 = (f32[8,30,720]{2,0,1:T(8,128)S(1)}, f32[8,30,720]{2,0,1:T(8,128)}, u32[]{:S(2)}) copy-start(f32[8,30,720]{2,0,1:T(8,128)} %param.9) | copy-start | bytes 2073604
  109.8 32.0 %copy-start.3 = (f32[8,30,720]{2,0,1:T(8,128)S(1)}, f32[8,30,720]{2,0,1:T(8,128)}, u32[]{:S(2)}) copy-start(f32[8,30,720]{2,0,1:T(8,128)} %param.8) | copy-start | bytes 2073604
